TPU v7x, 256 devices: a whole 4x4x8 slice. The times are simulated.
256 devices in a mesh: guide: 2 (over z_lo), seq: 32 (over x, y, core), tp: 4 (over z_hi).
Axes of the slice: x: 4, y: 4, z: 8 (z_hi: 4, z_lo: 2; z = z_hi * 2 + z_lo), core: 2. Of those that a mesh axis runs over, the one named last changes fastest.
Arguments:
- hidden: bfloat16 [2048, 3072], P('seq', 'tp'), may hold values from -6 to 6
- seg_ids: int32 [2048], P('seq'), may hold values from 0 to 3, never falling along the last dimension, each value on 1 to 769 neighbouring positions
- modulation: bfloat16 [2, 4, 3, 3072], P('guide'), may hold values from -4 to 4
- qk_gain: float32 [2, 128], replicated, may hold values from 0.5 to 5
- w_qkv: bfloat16 [3072, 3, 1536], P(None, None, 'tp'), may hold values from -0.109375 to 0.109375
- w_mlp_in: bfloat16 [3072, 6144], P('seq', 'tp'), may hold values from -0.109375 to 0.109375
- w_out: bfloat16 [1536, 3072], P('tp'), may hold values from -0.5 to 0.5
- w_mlp_back: bfloat16 [3072, 6144], P('seq', 'tp'), may hold values from -0.078125 to 0.078125
Outputs:
- guided: bfloat16 [2048, 4, 2, 384], P('seq', 'tp', 'guide')
Inputs may be any that keep to these rules, and one draw needn't show every extreme that they name: `seg_ids`: 4 requests lie end to end in order; each holds 1 to 769 rows and one holds exactly 769.
All inputs are finite; a program needn't handle non-finite values.
Results may differ from a plain program's by a relative error of at most 0.014.
The roundings to bfloat16 on the way count: a program that leaves them out, or rounds other values in their place, can miss the bound.
Values may be sent and summed in bfloat16 or wider, within the bound.
A program may use at most 128 MiB of HBM per device.

v0:
```python
import jax
import jax.numpy as jnp
from jax import lax
from jax.sharding import PartitionSpec as P

D = 3072
HEAD = 128


guidance = 3.5


def shifted(value, axis, by):
    devices = lax.axis_size(axis)
    pairs = [(i, i + by) for i in range(devices) if 0 <= i + by < devices]
    return lax.ppermute(value, axis, pairs)


def from_partner(block, axis, apart):
    count = lax.axis_size(axis)
    route = []
    for low in range(count):
        high = low | 1 << apart
        if high != low and high < count:
            route += [(low, high), (high, low)]
    return lax.ppermute(block, axis, route)


def head_norm(values, gain):
    return values * lax.rsqrt(jnp.mean(values * values, axis=-1, keepdims=True) + 1e-06) * gain


def on_device(hidden, seg_ids, modulation, qk_gain, w_qkv, w_mlp_in, w_out, w_mlp_back):
    rows = hidden.shape[0]
    local_width = hidden.shape[1]
    group = w_out.shape[0]
    heads_here = group // HEAD
    requests = modulation.shape[1]
    tp_index = lax.axis_index("tp")
    reach = min(lax.axis_size("seq") - 1, 12)
    full = lax.all_gather(hidden, "tp", axis=1, tiled=True)
    xf = full.astype(jnp.float32)
    centred = xf - jnp.mean(xf, axis=-1, keepdims=True)
    normed = centred * lax.rsqrt(jnp.mean(centred * centred, axis=-1, keepdims=True) + 1e-06)
    one_hot = (seg_ids[:, None] == lax.iota(jnp.int32, requests)[None, :]).astype(jnp.bfloat16)
    table = modulation[0, :, 0:2, :].reshape(requests, 2 * D)
    looked = jnp.dot(one_hot, table, preferred_element_type=jnp.float32)
    xmod = (normed * (1.0 + looked[:, D:]) + looked[:, :D]).astype(jnp.bfloat16)
    gate_table = lax.dynamic_slice_in_dim(
        modulation[0, :, 2, :], tp_index * local_width, local_width, 1
    )
    gate = jnp.dot(one_hot, gate_table, preferred_element_type=jnp.float32)
    mlp_pre = jnp.dot(
        xmod,
        lax.all_gather(w_mlp_in, "seq", axis=0, tiled=True),
        preferred_element_type=jnp.float32,
    )
    mlp_act = jax.nn.gelu(mlp_pre, approximate=True).astype(jnp.bfloat16)
    proj = jnp.einsum("td,dck->tck", xmod, w_qkv, preferred_element_type=jnp.float32)
    query = head_norm(proj[:, 0].reshape(rows, heads_here, HEAD), qk_gain[0]).astype(jnp.bfloat16)
    key_rows = head_norm(proj[:, 1].reshape(rows, heads_here, HEAD), qk_gain[1]).astype(
        jnp.bfloat16
    )
    value_rows = proj[:, 2].astype(jnp.bfloat16)
    packed = jnp.concatenate([key_rows.reshape(rows, group), value_rows], axis=1)
    seg_plus = seg_ids + 1

    def attend_block(state, kv_block, seg_block):
        peak, total, summed = state
        count = kv_block.shape[0]
        keys = kv_block[:, :group].reshape(count, heads_here, HEAD)
        values = kv_block[:, group:].reshape(count, heads_here, HEAD)
        score = jnp.einsum(
            "qhe,khe->hqk", query, keys, preferred_element_type=jnp.float32
        ) * HEAD ** (-0.5)
        score = jnp.where((seg_plus[:, None] == seg_block[None, :])[None], score, -1e30)
        new_peak = jnp.maximum(peak, jnp.max(score, axis=-1))
        factor = jnp.exp(peak - new_peak)
        weight = jnp.exp(score - new_peak[:, :, None])
        total = total * factor + jnp.sum(weight, axis=-1)
        summed = summed * factor[:, :, None] + jnp.einsum(
            "hqk,khe->hqe", weight.astype(jnp.bfloat16), values, preferred_element_type=jnp.float32
        )
        return (new_peak, total, summed)

    def absorb(state, kv_piece, seg_piece):
        blocks = kv_piece.shape[0] // rows

        def step(index, carry):
            return attend_block(carry, kv_piece, seg_piece)

        return lax.fori_loop(0, blocks, step, state)

    start_state = (
        jnp.full((heads_here, rows), -1e30, jnp.float32),
        jnp.zeros((heads_here, rows), jnp.float32),
        jnp.zeros((heads_here, rows, HEAD), jnp.float32),
    )
    first = absorb(start_state, packed, seg_plus)

    def turn(index, carry):
        state_now, lower, upper = carry
        lower = shifted((lower[0], lower[1]), "seq", 1)
        upper = shifted((upper[0], upper[1]), "seq", -1)
        state_now = absorb(state_now, lower[0], lower[1])
        state_now = absorb(state_now, upper[0], upper[1])
        return (state_now, lower, upper)

    state, unused_low, unused_high = lax.fori_loop(
        0, reach, turn, (first, (packed, seg_plus), (packed, seg_plus))
    )
    peak, total, summed = state
    attended = (summed / total[:, :, None]).astype(jnp.bfloat16)
    attended = jnp.transpose(attended, (1, 0, 2)).reshape(rows, group)
    mlp_term = lax.dot_general(
        mlp_act,
        lax.all_gather(w_mlp_back, "seq", axis=0, tiled=True),
        (((1,), (1,)), ((), ())),
        preferred_element_type=jnp.float32,
    )
    partial_term = jnp.dot(attended, w_out, preferred_element_type=jnp.float32) + mlp_term
    branch = lax.psum_scatter(
        partial_term.astype(jnp.bfloat16), "tp", scatter_dimension=1, tiled=True
    ).astype(jnp.float32)
    own_half = (hidden.astype(jnp.float32) + gate * branch).astype(jnp.bfloat16)
    split_width = local_width // 2
    guide_index = lax.axis_index("guide")
    kept = lax.dynamic_slice_in_dim(own_half, guide_index * split_width, split_width, 1)
    handed = lax.dynamic_slice_in_dim(own_half, (1 - guide_index) * split_width, split_width, 1)
    other_half = from_partner(handed, "guide", 0)
    is_cond = guide_index == 0
    cond = jnp.where(is_cond, kept, other_half).astype(jnp.float32)
    uncond = jnp.where(is_cond, other_half, kept).astype(jnp.float32)
    guided = (uncond + guidance * (cond - uncond)).astype(jnp.bfloat16)
    return guided.reshape(rows, 1, 1, split_width)


def solution(mesh):
    in_specs = (
        P("seq", "tp"),
        P("seq"),
        P("guide", None, None, None),
        P(),
        P(None, None, "tp"),
        P("seq", "tp"),
        P("tp", None),
        P("seq", "tp"),
    )
    out_specs = P("seq", "tp", "guide", None)
    return jax.shard_map(
        on_device, mesh=mesh, in_specs=in_specs, out_specs=out_specs, check_vma=False
    )
```

profile of v0, /device:TPU:4, one launch (start us, length us, event | category | flops | bytes accessed | tf_op | source)
XLA Modules:
  0.0 314.0 jit_solution(6634211180391683982)
XLA Ops:
  8.1 19.0 %all_gather.9 = bf16[64,3072]{1,0:T(8,128)(2,1)S(1)} all-gather(bf16[64,768]{1,0:T(8,128)(2,1)} %param.10), channel_id=1, replica_groups=mesh['guide'=2,'seq'=32,'tp'=4] {'tp'}, dimensions={1}, use_global_device_ids=true | all-gather | bytes 491520 | tf_op jit(solution)/shard_map/all_gather | solution.py:41
  30.3 4.4 %fusion.41 = f32[64,3,384]{2,0,1:T(8,128)S(1)} fusion(bf16[3072,3,384]{2,0,1:T(8,128)(2,1)} %param.14, bf16[64,3072]{1,0:T(8,128)(2,1)S(1)} %fusion.32), kind=kOutput, calls=%fused_computation.64 | convolution fusion | flops 452984832 | bytes 7766016 | tf_op jit(solution)/shard_map/td,dck->tck/dot_general | solution.py:59
  38.6 226.2 %while.4 = (s32[]{:T(128)}, f32[3,64]{1,0:T(4,128)S(1)}, f32[3,64]{1,0:T(4,128)S(1)}, f32[3,64,128]{2,1,0:T(8,128)S(1)}, bf16[64,768]{1,0:T(8,128)(2,1)S(1)}, /*...) while((s32[]{:T(128)}, f32[3,64]{1,0:T(4,128)S(1)}, ...), condition=%wide.region_11.12_spmd, body=%wide.region_6.11_spmd.sunk | while | flops 12911362 | bytes 2612749 | solution.py:109
  38.6 1.9 collective-permute-start
  40.6 5.8 %collective-permute-start.1 = (s32[64]{0:T(128)}, s32[64]{0:T(128)S(1)}, u32[]{:S(2)}, u32[]{:S(2)}) collective-permute-start(s32[64]{0:T(128)} %get-tuple-element.322), channel_id=1, source_target_pairs={{4,0},{8,4},{12,8},{16,12},{20,16},{24,20},{28,24},{32,28},{36,32}... | collective-permute-start | bytes 776 | tf_op jit(solution)/shard_map/while/body/eval_jaxpr/ppermute | solution.py:16
  46.3 1.9 collective-permute-start.2
  48.3 2.4 collective-permute-start.3
  52.6 5.8 %collective-permute-done.3 = bf16[64,768]{1,0:T(8,128)(2,1)S(1)} collective-permute-done((bf16[64,768]{1,0:T(8,128)(2,1)S(1)}, bf16[64,768]{1,0:T(8,128)(2,1)S(1)}, u32[]{:S(2)}, u32[]{:S(2)}) %collective-permute-start.3) | collective-permute-done | bytes 98336 | tf_op jit(solution)/shard_map/while/body/eval_jaxpr/ppermute | solution.py:16
  59.2 1.9 collective-permute-start
  61.1 5.8 %collective-permute-start.1 = (s32[64]{0:T(128)}, s32[64]{0:T(128)S(1)}, u32[]{:S(2)}, u32[]{:S(2)}) collective-permute-start(s32[64]{0:T(128)} %get-tuple-element.322), channel_id=1, source_target_pairs={{4,0},{8,4},{12,8},{16,12},{20,16},{24,20},{28,24},{32,28},{36,32}... | collective-permute-start | bytes 776 | tf_op jit(solution)/shard_map/while/body/eval_jaxpr/ppermute | solution.py:16
  66.9 1.9 collective-permute-start.2
  68.8 2.4 collective-permute-start.3
  72.6 4.3 %collective-permute-done.3 = bf16[64,768]{1,0:T(8,128)(2,1)S(1)} collective-permute-done((bf16[64,768]{1,0:T(8,128)(2,1)S(1)}, bf16[64,768]{1,0:T(8,128)(2,1)S(1)}, u32[]{:S(2)}, u32[]{:S(2)}) %collective-permute-start.3) | collective-permute-done | bytes 98336 | tf_op jit(solution)/shard_map/while/body/eval_jaxpr/ppermute | solution.py:16
  77.6 1.9 collective-permute-start
  79.6 5.8 %collective-permute-start.1 = (s32[64]{0:T(128)}, s32[64]{0:T(128)S(1)}, u32[]{:S(2)}, u32[]{:S(2)}) collective-permute-start(s32[64]{0:T(128)} %get-tuple-element.322), channel_id=1, source_target_pairs={{4,0},{8,4},{12,8},{16,12},{20,16},{24,20},{28,24},{32,28},{36,32}... | collective-permute-start | bytes 776 | tf_op jit(solution)/shard_map/while/body/eval_jaxpr/ppermute | solution.py:16
  85.3 1.9 collective-permute-start.2
  87.2 2.4 collective-permute-start.3
  91.0 4.9 %collective-permute-done.3 = bf16[64,768]{1,0:T(8,128)(2,1)S(1)} collective-permute-done((bf16[64,768]{1,0:T(8,128)(2,1)S(1)}, bf16[64,768]{1,0:T(8,128)(2,1)S(1)}, u32[]{:S(2)}, u32[]{:S(2)}) %collective-permute-start.3) | collective-permute-done | bytes 98336 | tf_op jit(solution)/shard_map/while/body/eval_jaxpr/ppermute | solution.py:16
  96.7 1.9 collective-permute-start
  98.6 5.8 %collective-permute-start.1 = (s32[64]{0:T(128)}, s32[64]{0:T(128)S(1)}, u32[]{:S(2)}, u32[]{:S(2)}) collective-permute-start(s32[64]{0:T(128)} %get-tuple-element.322), channel_id=1, source_target_pairs={{4,0},{8,4},{12,8},{16,12},{20,16},{24,20},{28,24},{32,28},{36,32}... | collective-permute-start | bytes 776 | tf_op jit(solution)/shard_map/while/body/eval_jaxpr/ppermute | solution.py:16
  104.4 1.9 collective-permute-start.2
  106.3 2.4 collective-permute-start.3
  110.1 4.3 %collective-permute-done.3 = bf16[64,768]{1,0:T(8,128)(2,1)S(1)} collective-permute-done((bf16[64,768]{1,0:T(8,128)(2,1)S(1)}, bf16[64,768]{1,0:T(8,128)(2,1)S(1)}, u32[]{:S(2)}, u32[]{:S(2)}) %collective-permute-start.3) | collective-permute-done | bytes 98336 | tf_op jit(solution)/shard_map/while/body/eval_jaxpr/ppermute | solution.py:16
  115.2 1.9 collective-permute-start
  117.1 5.8 %collective-permute-start.1 = (s32[64]{0:T(128)}, s32[64]{0:T(128)S(1)}, u32[]{:S(2)}, u32[]{:S(2)}) collective-permute-start(s32[64]{0:T(128)} %get-tuple-element.322), channel_id=1, source_target_pairs={{4,0},{8,4},{12,8},{16,12},{20,16},{24,20},{28,24},{32,28},{36,32}... | collective-permute-start | bytes 776 | tf_op jit(solution)/shard_map/while/body/eval_jaxpr/ppermute | solution.py:16
  122.9 1.9 collective-permute-start.2
  124.8 2.4 collective-permute-start.3
  129.2 5.7 %collective-permute-done.3 = bf16[64,768]{1,0:T(8,128)(2,1)S(1)} collective-permute-done((bf16[64,768]{1,0:T(8,128)(2,1)S(1)}, bf16[64,768]{1,0:T(8,128)(2,1)S(1)}, u32[]{:S(2)}, u32[]{:S(2)}) %collective-permute-start.3) | collective-permute-done | bytes 98336 | tf_op jit(solution)/shard_map/while/body/eval_jaxpr/ppermute | solution.py:16
  135.7 1.9 collective-permute-start
  137.6 5.8 %collective-permute-start.1 = (s32[64]{0:T(128)}, s32[64]{0:T(128)S(1)}, u32[]{:S(2)}, u32[]{:S(2)}) collective-permute-start(s32[64]{0:T(128)} %get-tuple-element.322), channel_id=1, source_target_pairs={{4,0},{8,4},{12,8},{16,12},{20,16},{24,20},{28,24},{32,28},{36,32}... | collective-permute-start | bytes 776 | tf_op jit(solution)/shard_map/while/body/eval_jaxpr/ppermute | solution.py:16
  143.4 1.9 collective-permute-start.2
  145.3 2.4 collective-permute-start.3
  149.1 4.3 %collective-permute-done.3 = bf16[64,768]{1,0:T(8,128)(2,1)S(1)} collective-permute-done((bf16[64,768]{1,0:T(8,128)(2,1)S(1)}, bf16[64,768]{1,0:T(8,128)(2,1)S(1)}, u32[]{:S(2)}, u32[]{:S(2)}) %collective-permute-start.3) | collective-permute-done | bytes 98336 | tf_op jit(solution)/shard_map/while/body/eval_jaxpr/ppermute | solution.py:16
  154.2 1.9 collective-permute-start
  156.1 5.8 %collective-permute-start.1 = (s32[64]{0:T(128)}, s32[64]{0:T(128)S(1)}, u32[]{:S(2)}, u32[]{:S(2)}) collective-permute-start(s32[64]{0:T(128)} %get-tuple-element.322), channel_id=1, source_target_pairs={{4,0},{8,4},{12,8},{16,12},{20,16},{24,20},{28,24},{32,28},{36,32}... | collective-permute-start | bytes 776 | tf_op jit(solution)/shard_map/while/body/eval_jaxpr/ppermute | solution.py:16
  161.8 1.9 collective-permute-start.2
  163.8 2.4 collective-permute-start.3
  167.5 4.3 %collective-permute-done.3 = bf16[64,768]{1,0:T(8,128)(2,1)S(1)} collective-permute-done((bf16[64,768]{1,0:T(8,128)(2,1)S(1)}, bf16[64,768]{1,0:T(8,128)(2,1)S(1)}, u32[]{:S(2)}, u32[]{:S(2)}) %collective-permute-start.3) | collective-permute-done | bytes 98336 | tf_op jit(solution)/shard_map/while/body/eval_jaxpr/ppermute | solution.py:16
  172.6 1.9 collective-permute-start
  174.5 5.8 %collective-permute-start.1 = (s32[64]{0:T(128)}, s32[64]{0:T(128)S(1)}, u32[]{:S(2)}, u32[]{:S(2)}) collective-permute-start(s32[64]{0:T(128)} %get-tuple-element.322), channel_id=1, source_target_pairs={{4,0},{8,4},{12,8},{16,12},{20,16},{24,20},{28,24},{32,28},{36,32}... | collective-permute-start | bytes 776 | tf_op jit(solution)/shard_map/while/body/eval_jaxpr/ppermute | solution.py:16
  180.3 1.9 collective-permute-start.2
  182.2 2.4 collective-permute-start.3
  186.0 4.3 %collective-permute-done.3 = bf16[64,768]{1,0:T(8,128)(2,1)S(1)} collective-permute-done((bf16[64,768]{1,0:T(8,128)(2,1)S(1)}, bf16[64,768]{1,0:T(8,128)(2,1)S(1)}, u32[]{:S(2)}, u32[]{:S(2)}) %collective-permute-start.3) | collective-permute-done | bytes 98336 | tf_op jit(solution)/shard_map/while/body/eval_jaxpr/ppermute | solution.py:16
  191.1 1.9 collective-permute-start
  193.0 5.8 %collective-permute-start.1 = (s32[64]{0:T(128)}, s32[64]{0:T(128)S(1)}, u32[]{:S(2)}, u32[]{:S(2)}) collective-permute-start(s32[64]{0:T(128)} %get-tuple-element.322), channel_id=1, source_target_pairs={{4,0},{8,4},{12,8},{16,12},{20,16},{24,20},{28,24},{32,28},{36,32}... | collective-permute-start | bytes 776 | tf_op jit(solution)/shard_map/while/body/eval_jaxpr/ppermute | solution.py:16
  198.8 1.9 collective-permute-start.2
  200.7 2.4 collective-permute-start.3
  204.4 4.3 %collective-permute-done.3 = bf16[64,768]{1,0:T(8,128)(2,1)S(1)} collective-permute-done((bf16[64,768]{1,0:T(8,128)(2,1)S(1)}, bf16[64,768]{1,0:T(8,128)(2,1)S(1)}, u32[]{:S(2)}, u32[]{:S(2)}) %collective-permute-start.3) | collective-permute-done | bytes 98336 | tf_op jit(solution)/shard_map/while/body/eval_jaxpr/ppermute | solution.py:16
  209.5 1.9 collective-permute-start
  211.4 5.8 %collective-permute-start.1 = (s32[64]{0:T(128)}, s32[64]{0:T(128)S(1)}, u32[]{:S(2)}, u32[]{:S(2)}) collective-permute-start(s32[64]{0:T(128)} %get-tuple-element.322), channel_id=1, source_target_pairs={{4,0},{8,4},{12,8},{16,12},{20,16},{24,20},{28,24},{32,28},{36,32}... | collective-permute-start | bytes 776 | tf_op jit(solution)/shard_map/while/body/eval_jaxpr/ppermute | solution.py:16
  217.2 1.9 collective-permute-start.2
  219.1 2.4 collective-permute-start.3
  222.9 4.3 %collective-permute-done.3 = bf16[64,768]{1,0:T(8,128)(2,1)S(1)} collective-permute-done((bf16[64,768]{1,0:T(8,128)(2,1)S(1)}, bf16[64,768]{1,0:T(8,128)(2,1)S(1)}, u32[]{:S(2)}, u32[]{:S(2)}) %collective-permute-start.3) | collective-permute-done | bytes 98336 | tf_op jit(solution)/shard_map/while/body/eval_jaxpr/ppermute | solution.py:16
  229.9 5.8 %collective-permute-start.1 = (s32[64]{0:T(128)}, s32[64]{0:T(128)S(1)}, u32[]{:S(2)}, u32[]{:S(2)}) collective-permute-start(s32[64]{0:T(128)} %get-tuple-element.322), channel_id=1, source_target_pairs={{4,0},{8,4},{12,8},{16,12},{20,16},{24,20},{28,24},{32,28},{36,32}... | collective-permute-start | bytes 776 | tf_op jit(solution)/shard_map/while/body/eval_jaxpr/ppermute | solution.py:16
  235.7 1.9 collective-permute-start.2
  237.6 2.4 collective-permute-start.3
  241.4 4.3 %collective-permute-done.3 = bf16[64,768]{1,0:T(8,128)(2,1)S(1)} collective-permute-done((bf16[64,768]{1,0:T(8,128)(2,1)S(1)}, bf16[64,768]{1,0:T(8,128)(2,1)S(1)}, u32[]{:S(2)}, u32[]{:S(2)}) %collective-permute-start.3) | collective-permute-done | bytes 98336 | tf_op jit(solution)/shard_map/while/body/eval_jaxpr/ppermute | solution.py:16
  248.4 5.8 %collective-permute-start.1 = (s32[64]{0:T(128)}, s32[64]{0:T(128)S(1)}, u32[]{:S(2)}, u32[]{:S(2)}) collective-permute-start(s32[64]{0:T(128)} %get-tuple-element.322), channel_id=1, source_target_pairs={{4,0},{8,4},{12,8},{16,12},{20,16},{24,20},{28,24},{32,28},{36,32}... | collective-permute-start | bytes 776 | tf_op jit(solution)/shard_map/while/body/eval_jaxpr/ppermute | solution.py:16
  254.1 1.9 collective-permute-start.2
  256.0 2.4 collective-permute-start.3
  259.8 4.3 %collective-permute-done.3 = bf16[64,768]{1,0:T(8,128)(2,1)S(1)} collective-permute-done((bf16[64,768]{1,0:T(8,128)(2,1)S(1)}, bf16[64,768]{1,0:T(8,128)(2,1)S(1)}, u32[]{:S(2)}, u32[]{:S(2)}) %collective-permute-start.3) | collective-permute-done | bytes 98336 | tf_op jit(solution)/shard_map/while/body/eval_jaxpr/ppermute | solution.py:16
  266.4 11.9 %fusion.23 = bf16[64,3072]{1,0:T(8,128)(2,1)} fusion(f32[64,3072]{1,0:T(8,128)} %fusion.56, bf16[3072,1536]{1,0:T(8,128)(2,1)} %all-gather.5.cloned.1.call-done, bf16[64,3072]{1,0:T(8,128)(2,1)S(1)} %fusion.32, bf16[3072,1536]{1,0:T(8,128)(2,1)} %all-gather.3.cloned.1.call-done), kind=kOutput, calls=%fused_computation.39 | convolution fusion | flops 1209237504 | bytes 20447232 | tf_op jit(solution)/shard_map/dot_general | solution.py:115
  278.3 23.1 %reduce-scatter.2.cloned.1.call-done = bf16[64,768]{1,0:T(8,128)(2,1)} async-done(((bf16[64,3072]{1,0:T(8,128)(2,1)}), bf16[64,768]{1,0:T(8,128)(2,1)}) %reduce-scatter.2.cloned.1.call-update) | async-done | bytes 98320 | tf_op jit(solution)/shard_map/reduce_scatter | solution.py:122
  303.2 3.6 %collective-permute-done.4 = bf16[64,384]{1,0:T(8,128)(2,1)S(1)} collective-permute-done((bf16[64,384]{1,0:T(8,128)(2,1)S(1)}, bf16[64,384]{1,0:T(8,128)(2,1)S(1)}, u32[]{:S(2)}, u32[]{:S(2)}) %collective-permute-start.4) | collective-permute-done | bytes 49184 | tf_op jit(solution)/shard_map/ppermute | solution.py:26
  (275 shorter events, 42.2 us)
Async XLA Ops:
  6.5 258.3 %copy-start = (bf16[384,3072]{1,0:T(8,128)(2,1)S(1)}, bf16[384,3072]{1,0:T(8,128)(2,1)}, u32[]{:S(2)}) copy-start(bf16[384,3072]{1,0:T(8,128)(2,1)} %param.16) | copy-start | bytes 7077892
  6.5 259.9 %all-gather.3.cloned.1.call-start = ((), (), s32[]{:S(2)}) async-start(), calls=%async_computation.1 | async-start | bytes 9732096 | tf_op jit(solution)/shard_map/all_gather | solution.py:55
  7.3 259.2 %all-gather.5.cloned.1.call-start = ((), (), s32[]{:S(2)}) async-start(), calls=%async_computation.2 | async-start | bytes 9732096 | tf_op jit(solution)/shard_map/all_gather | solution.py:117
  8.0 293.5 %reduce-scatter.2.cloned.1.call-start = ((), (), s32[]{:S(2)}) async-start(), calls=%async_computation.3 | async-start | bytes 491520 | tf_op jit(solution)/shard_map/reduce_scatter | solution.py:122
  27.0 9.9 %copy-start.3 = (f32[2,128]{1,0:T(2,128)S(1)}, f32[2,128]{1,0:T(2,128)}, u32[]{:S(2)}) copy-start(f32[2,128]{1,0:T(2,128)} %param.13) | copy-start | bytes 3076
  38.6 12.0 %collective-permute-start = (s32[64]{0:T(128)}, s32[64]{0:T(128)S(1)}, u32[]{:S(2)}, u32[]{:S(2)}) collective-permute-start(s32[64]{0:T(128)} %get-tuple-element.320), channel_id=1, source_target_pairs={{0,4},{4,8},{8,12},{12,16},{16,20},{20,24},{24,28},{28,32},{32,36}... | collective-permute-start | bytes 776 | tf_op jit(solution)/shard_map/while/body/eval_jaxpr/ppermute | solution.py:16
  40.6 10.1 %collective-permute-start.1 = (s32[64]{0:T(128)}, s32[64]{0:T(128)S(1)}, u32[]{:S(2)}, u32[]{:S(2)}) collective-permute-start(s32[64]{0:T(128)} %get-tuple-element.322), channel_id=1, source_target_pairs={{4,0},{8,4},{12,8},{16,12},{20,16},{24,20},{28,24},{32,28},{36,32}... | collective-permute-start | bytes 776 | tf_op jit(solution)/shard_map/while/body/eval_jaxpr/ppermute | solution.py:16
  46.3 6.1 %collective-permute-start.2 = (bf16[64,768]{1,0:T(8,128)(2,1)S(1)}, bf16[64,768]{1,0:T(8,128)(2,1)S(1)}, u32[]{:S(2)}, u32[]{:S(2)}) collective-permute-start(bf16[64,768]{1,0:T(8,128)(2,1)S(1)} %get-tuple-element.321), channel_id=1, source_target_pairs={{4,0},{8,4},{12,8},{16,12},{20,16},{24,20},{28,24},{32,28},{36,32}... | collective-permute-start | bytes 294920 | tf_op jit(solution)/shard_map/while/body/eval_jaxpr/ppermute | solution.py:16
  48.3 10.1 %collective-permute-start.3 = (bf16[64,768]{1,0:T(8,128)(2,1)S(1)}, bf16[64,768]{1,0:T(8,128)(2,1)S(1)}, u32[]{:S(2)}, u32[]{:S(2)}) collective-permute-start(bf16[64,768]{1,0:T(8,128)(2,1)S(1)} %get-tuple-element.319), channel_id=1, source_target_pairs={{0,4},{4,8},{8,12},{12,16},{16,20},{20,24},{24,28},{28,32},{32,36}... | collective-permute-start | bytes 294920 | tf_op jit(solution)/shard_map/while/body/eval_jaxpr/ppermute | solution.py:16
  59.2 12.0 %collective-permute-start = (s32[64]{0:T(128)}, s32[64]{0:T(128)S(1)}, u32[]{:S(2)}, u32[]{:S(2)}) collective-permute-start(s32[64]{0:T(128)} %get-tuple-element.320), channel_id=1, source_target_pairs={{0,4},{4,8},{8,12},{12,16},{16,20},{20,24},{24,28},{28,32},{32,36}... | collective-permute-start | bytes 776 | tf_op jit(solution)/shard_map/while/body/eval_jaxpr/ppermute | solution.py:16
  61.1 10.1 %collective-permute-start.1 = (s32[64]{0:T(128)}, s32[64]{0:T(128)S(1)}, u32[]{:S(2)}, u32[]{:S(2)}) collective-permute-start(s32[64]{0:T(128)} %get-tuple-element.322), channel_id=1, source_target_pairs={{4,0},{8,4},{12,8},{16,12},{20,16},{24,20},{28,24},{32,28},{36,32}... | collective-permute-start | bytes 776 | tf_op jit(solution)/shard_map/while/body/eval_jaxpr/ppermute | solution.py:16
  66.9 5.5 %collective-permute-start.2 = (bf16[64,768]{1,0:T(8,128)(2,1)S(1)}, bf16[64,768]{1,0:T(8,128)(2,1)S(1)}, u32[]{:S(2)}, u32[]{:S(2)}) collective-permute-start(bf16[64,768]{1,0:T(8,128)(2,1)S(1)} %get-tuple-element.321), channel_id=1, source_target_pairs={{4,0},{8,4},{12,8},{16,12},{20,16},{24,20},{28,24},{32,28},{36,32}... | collective-permute-start | bytes 294920 | tf_op jit(solution)/shard_map/while/body/eval_jaxpr/ppermute | solution.py:16
  68.8 8.0 %collective-permute-start.3 = (bf16[64,768]{1,0:T(8,128)(2,1)S(1)}, bf16[64,768]{1,0:T(8,128)(2,1)S(1)}, u32[]{:S(2)}, u32[]{:S(2)}) collective-permute-start(bf16[64,768]{1,0:T(8,128)(2,1)S(1)} %get-tuple-element.319), channel_id=1, source_target_pairs={{0,4},{4,8},{8,12},{12,16},{16,20},{20,24},{24,28},{28,32},{32,36}... | collective-permute-start | bytes 294920 | tf_op jit(solution)/shard_map/while/body/eval_jaxpr/ppermute | solution.py:16
  77.6 12.0 %collective-permute-start = (s32[64]{0:T(128)}, s32[64]{0:T(128)S(1)}, u32[]{:S(2)}, u32[]{:S(2)}) collective-permute-start(s32[64]{0:T(128)} %get-tuple-element.320), channel_id=1, source_target_pairs={{0,4},{4,8},{8,12},{12,16},{16,20},{20,24},{24,28},{28,32},{32,36}... | collective-permute-start | bytes 776 | tf_op jit(solution)/shard_map/while/body/eval_jaxpr/ppermute | solution.py:16
  79.6 10.1 %collective-permute-start.1 = (s32[64]{0:T(128)}, s32[64]{0:T(128)S(1)}, u32[]{:S(2)}, u32[]{:S(2)}) collective-permute-start(s32[64]{0:T(128)} %get-tuple-element.322), channel_id=1, source_target_pairs={{4,0},{8,4},{12,8},{16,12},{20,16},{24,20},{28,24},{32,28},{36,32}... | collective-permute-start | bytes 776 | tf_op jit(solution)/shard_map/while/body/eval_jaxpr/ppermute | solution.py:16
  85.3 5.5 %collective-permute-start.2 = (bf16[64,768]{1,0:T(8,128)(2,1)S(1)}, bf16[64,768]{1,0:T(8,128)(2,1)S(1)}, u32[]{:S(2)}, u32[]{:S(2)}) collective-permute-start(bf16[64,768]{1,0:T(8,128)(2,1)S(1)} %get-tuple-element.321), channel_id=1, source_target_pairs={{4,0},{8,4},{12,8},{16,12},{20,16},{24,20},{28,24},{32,28},{36,32}... | collective-permute-start | bytes 294920 | tf_op jit(solution)/shard_map/while/body/eval_jaxpr/ppermute | solution.py:16
  87.2 8.7 %collective-permute-start.3 = (bf16[64,768]{1,0:T(8,128)(2,1)S(1)}, bf16[64,768]{1,0:T(8,128)(2,1)S(1)}, u32[]{:S(2)}, u32[]{:S(2)}) collective-permute-start(bf16[64,768]{1,0:T(8,128)(2,1)S(1)} %get-tuple-element.319), channel_id=1, source_target_pairs={{0,4},{4,8},{8,12},{12,16},{16,20},{20,24},{24,28},{28,32},{32,36}... | collective-permute-start | bytes 294920 | tf_op jit(solution)/shard_map/while/body/eval_jaxpr/ppermute | solution.py:16
  96.7 12.0 %collective-permute-start = (s32[64]{0:T(128)}, s32[64]{0:T(128)S(1)}, u32[]{:S(2)}, u32[]{:S(2)}) collective-permute-start(s32[64]{0:T(128)} %get-tuple-element.320), channel_id=1, source_target_pairs={{0,4},{4,8},{8,12},{12,16},{16,20},{20,24},{24,28},{28,32},{32,36}... | collective-permute-start | bytes 776 | tf_op jit(solution)/shard_map/while/body/eval_jaxpr/ppermute | solution.py:16
  98.6 10.1 %collective-permute-start.1 = (s32[64]{0:T(128)}, s32[64]{0:T(128)S(1)}, u32[]{:S(2)}, u32[]{:S(2)}) collective-permute-start(s32[64]{0:T(128)} %get-tuple-element.322), channel_id=1, source_target_pairs={{4,0},{8,4},{12,8},{16,12},{20,16},{24,20},{28,24},{32,28},{36,32}... | collective-permute-start | bytes 776 | tf_op jit(solution)/shard_map/while/body/eval_jaxpr/ppermute | solution.py:16
  104.4 5.5 %collective-permute-start.2 = (bf16[64,768]{1,0:T(8,128)(2,1)S(1)}, bf16[64,768]{1,0:T(8,128)(2,1)S(1)}, u32[]{:S(2)}, u32[]{:S(2)}) collective-permute-start(bf16[64,768]{1,0:T(8,128)(2,1)S(1)} %get-tuple-element.321), channel_id=1, source_target_pairs={{4,0},{8,4},{12,8},{16,12},{20,16},{24,20},{28,24},{32,28},{36,32}... | collective-permute-start | bytes 294920 | tf_op jit(solution)/shard_map/while/body/eval_jaxpr/ppermute | solution.py:16
  106.3 8.0 %collective-permute-start.3 = (bf16[64,768]{1,0:T(8,128)(2,1)S(1)}, bf16[64,768]{1,0:T(8,128)(2,1)S(1)}, u32[]{:S(2)}, u32[]{:S(2)}) collective-permute-start(bf16[64,768]{1,0:T(8,128)(2,1)S(1)} %get-tuple-element.319), channel_id=1, source_target_pairs={{0,4},{4,8},{8,12},{12,16},{16,20},{20,24},{24,28},{28,32},{32,36}... | collective-permute-start | bytes 294920 | tf_op jit(solution)/shard_map/while/body/eval_jaxpr/ppermute | solution.py:16
  115.2 12.0 %collective-permute-start = (s32[64]{0:T(128)}, s32[64]{0:T(128)S(1)}, u32[]{:S(2)}, u32[]{:S(2)}) collective-permute-start(s32[64]{0:T(128)} %get-tuple-element.320), channel_id=1, source_target_pairs={{0,4},{4,8},{8,12},{12,16},{16,20},{20,24},{24,28},{28,32},{32,36}... | collective-permute-start | bytes 776 | tf_op jit(solution)/shard_map/while/body/eval_jaxpr/ppermute | solution.py:16
  117.1 10.1 %collective-permute-start.1 = (s32[64]{0:T(128)}, s32[64]{0:T(128)S(1)}, u32[]{:S(2)}, u32[]{:S(2)}) collective-permute-start(s32[64]{0:T(128)} %get-tuple-element.322), channel_id=1, source_target_pairs={{4,0},{8,4},{12,8},{16,12},{20,16},{24,20},{28,24},{32,28},{36,32}... | collective-permute-start | bytes 776 | tf_op jit(solution)/shard_map/while/body/eval_jaxpr/ppermute | solution.py:16
  122.9 6.1 %collective-permute-start.2 = (bf16[64,768]{1,0:T(8,128)(2,1)S(1)}, bf16[64,768]{1,0:T(8,128)(2,1)S(1)}, u32[]{:S(2)}, u32[]{:S(2)}) collective-permute-start(bf16[64,768]{1,0:T(8,128)(2,1)S(1)} %get-tuple-element.321), channel_id=1, source_target_pairs={{4,0},{8,4},{12,8},{16,12},{20,16},{24,20},{28,24},{32,28},{36,32}... | collective-permute-start | bytes 294920 | tf_op jit(solution)/shard_map/while/body/eval_jaxpr/ppermute | solution.py:16
  124.8 10.1 %collective-permute-start.3 = (bf16[64,768]{1,0:T(8,128)(2,1)S(1)}, bf16[64,768]{1,0:T(8,128)(2,1)S(1)}, u32[]{:S(2)}, u32[]{:S(2)}) collective-permute-start(bf16[64,768]{1,0:T(8,128)(2,1)S(1)} %get-tuple-element.319), channel_id=1, source_target_pairs={{0,4},{4,8},{8,12},{12,16},{16,20},{20,24},{24,28},{28,32},{32,36}... | collective-permute-start | bytes 294920 | tf_op jit(solution)/shard_map/while/body/eval_jaxpr/ppermute | solution.py:16
  135.7 12.0 %collective-permute-start = (s32[64]{0:T(128)}, s32[64]{0:T(128)S(1)}, u32[]{:S(2)}, u32[]{:S(2)}) collective-permute-start(s32[64]{0:T(128)} %get-tuple-element.320), channel_id=1, source_target_pairs={{0,4},{4,8},{8,12},{12,16},{16,20},{20,24},{24,28},{28,32},{32,36}... | collective-permute-start | bytes 776 | tf_op jit(solution)/shard_map/while/body/eval_jaxpr/ppermute | solution.py:16
  137.6 10.1 %collective-permute-start.1 = (s32[64]{0:T(128)}, s32[64]{0:T(128)S(1)}, u32[]{:S(2)}, u32[]{:S(2)}) collective-permute-start(s32[64]{0:T(128)} %get-tuple-element.322), channel_id=1, source_target_pairs={{4,0},{8,4},{12,8},{16,12},{20,16},{24,20},{28,24},{32,28},{36,32}... | collective-permute-start | bytes 776 | tf_op jit(solution)/shard_map/while/body/eval_jaxpr/ppermute | solution.py:16
  143.4 5.5 %collective-permute-start.2 = (bf16[64,768]{1,0:T(8,128)(2,1)S(1)}, bf16[64,768]{1,0:T(8,128)(2,1)S(1)}, u32[]{:S(2)}, u32[]{:S(2)}) collective-permute-start(bf16[64,768]{1,0:T(8,128)(2,1)S(1)} %get-tuple-element.321), channel_id=1, source_target_pairs={{4,0},{8,4},{12,8},{16,12},{20,16},{24,20},{28,24},{32,28},{36,32}... | collective-permute-start | bytes 294920 | tf_op jit(solution)/shard_map/while/body/eval_jaxpr/ppermute | solution.py:16
  145.3 8.0 %collective-permute-start.3 = (bf16[64,768]{1,0:T(8,128)(2,1)S(1)}, bf16[64,768]{1,0:T(8,128)(2,1)S(1)}, u32[]{:S(2)}, u32[]{:S(2)}) collective-permute-start(bf16[64,768]{1,0:T(8,128)(2,1)S(1)} %get-tuple-element.319), channel_id=1, source_target_pairs={{0,4},{4,8},{8,12},{12,16},{16,20},{20,24},{24,28},{28,32},{32,36}... | collective-permute-start | bytes 294920 | tf_op jit(solution)/shard_map/while/body/eval_jaxpr/ppermute | solution.py:16
  154.2 12.0 %collective-permute-start = (s32[64]{0:T(128)}, s32[64]{0:T(128)S(1)}, u32[]{:S(2)}, u32[]{:S(2)}) collective-permute-start(s32[64]{0:T(128)} %get-tuple-element.320), channel_id=1, source_target_pairs={{0,4},{4,8},{8,12},{12,16},{16,20},{20,24},{24,28},{28,32},{32,36}... | collective-permute-start | bytes 776 | tf_op jit(solution)/shard_map/while/body/eval_jaxpr/ppermute | solution.py:16
  156.1 10.1 %collective-permute-start.1 = (s32[64]{0:T(128)}, s32[64]{0:T(128)S(1)}, u32[]{:S(2)}, u32[]{:S(2)}) collective-permute-start(s32[64]{0:T(128)} %get-tuple-element.322), channel_id=1, source_target_pairs={{4,0},{8,4},{12,8},{16,12},{20,16},{24,20},{28,24},{32,28},{36,32}... | collective-permute-start | bytes 776 | tf_op jit(solution)/shard_map/while/body/eval_jaxpr/ppermute | solution.py:16
  161.8 5.5 %collective-permute-start.2 = (bf16[64,768]{1,0:T(8,128)(2,1)S(1)}, bf16[64,768]{1,0:T(8,128)(2,1)S(1)}, u32[]{:S(2)}, u32[]{:S(2)}) collective-permute-start(bf16[64,768]{1,0:T(8,128)(2,1)S(1)} %get-tuple-element.321), channel_id=1, source_target_pairs={{4,0},{8,4},{12,8},{16,12},{20,16},{24,20},{28,24},{32,28},{36,32}... | collective-permute-start | bytes 294920 | tf_op jit(solution)/shard_map/while/body/eval_jaxpr/ppermute | solution.py:16
  163.8 8.0 %collective-permute-start.3 = (bf16[64,768]{1,0:T(8,128)(2,1)S(1)}, bf16[64,768]{1,0:T(8,128)(2,1)S(1)}, u32[]{:S(2)}, u32[]{:S(2)}) collective-permute-start(bf16[64,768]{1,0:T(8,128)(2,1)S(1)} %get-tuple-element.319), channel_id=1, source_target_pairs={{0,4},{4,8},{8,12},{12,16},{16,20},{20,24},{24,28},{28,32},{32,36}... | collective-permute-start | bytes 294920 | tf_op jit(solution)/shard_map/while/body/eval_jaxpr/ppermute | solution.py:16
  172.6 12.0 %collective-permute-start = (s32[64]{0:T(128)}, s32[64]{0:T(128)S(1)}, u32[]{:S(2)}, u32[]{:S(2)}) collective-permute-start(s32[64]{0:T(128)} %get-tuple-element.320), channel_id=1, source_target_pairs={{0,4},{4,8},{8,12},{12,16},{16,20},{20,24},{24,28},{28,32},{32,36}... | collective-permute-start | bytes 776 | tf_op jit(solution)/shard_map/while/body/eval_jaxpr/ppermute | solution.py:16
  174.5 10.1 %collective-permute-start.1 = (s32[64]{0:T(128)}, s32[64]{0:T(128)S(1)}, u32[]{:S(2)}, u32[]{:S(2)}) collective-permute-start(s32[64]{0:T(128)} %get-tuple-element.322), channel_id=1, source_target_pairs={{4,0},{8,4},{12,8},{16,12},{20,16},{24,20},{28,24},{32,28},{36,32}... | collective-permute-start | bytes 776 | tf_op jit(solution)/shard_map/while/body/eval_jaxpr/ppermute | solution.py:16
  180.3 5.5 %collective-permute-start.2 = (bf16[64,768]{1,0:T(8,128)(2,1)S(1)}, bf16[64,768]{1,0:T(8,128)(2,1)S(1)}, u32[]{:S(2)}, u32[]{:S(2)}) collective-permute-start(bf16[64,768]{1,0:T(8,128)(2,1)S(1)} %get-tuple-element.321), channel_id=1, source_target_pairs={{4,0},{8,4},{12,8},{16,12},{20,16},{24,20},{28,24},{32,28},{36,32}... | collective-permute-start | bytes 294920 | tf_op jit(solution)/shard_map/while/body/eval_jaxpr/ppermute | solution.py:16
  182.2 8.0 %collective-permute-start.3 = (bf16[64,768]{1,0:T(8,128)(2,1)S(1)}, bf16[64,768]{1,0:T(8,128)(2,1)S(1)}, u32[]{:S(2)}, u32[]{:S(2)}) collective-permute-start(bf16[64,768]{1,0:T(8,128)(2,1)S(1)} %get-tuple-element.319), channel_id=1, source_target_pairs={{0,4},{4,8},{8,12},{12,16},{16,20},{20,24},{24,28},{28,32},{32,36}... | collective-permute-start | bytes 294920 | tf_op jit(solution)/shard_map/while/body/eval_jaxpr/ppermute | solution.py:16
  191.1 12.0 %collective-permute-start = (s32[64]{0:T(128)}, s32[64]{0:T(128)S(1)}, u32[]{:S(2)}, u32[]{:S(2)}) collective-permute-start(s32[64]{0:T(128)} %get-tuple-element.320), channel_id=1, source_target_pairs={{0,4},{4,8},{8,12},{12,16},{16,20},{20,24},{24,28},{28,32},{32,36}... | collective-permute-start | bytes 776 | tf_op jit(solution)/shard_map/while/body/eval_jaxpr/ppermute | solution.py:16
  193.0 10.1 %collective-permute-start.1 = (s32[64]{0:T(128)}, s32[64]{0:T(128)S(1)}, u32[]{:S(2)}, u32[]{:S(2)}) collective-permute-start(s32[64]{0:T(128)} %get-tuple-element.322), channel_id=1, source_target_pairs={{4,0},{8,4},{12,8},{16,12},{20,16},{24,20},{28,24},{32,28},{36,32}... | collective-permute-start | bytes 776 | tf_op jit(solution)/shard_map/while/body/eval_jaxpr/ppermute | solution.py:16
  198.8 5.5 %collective-permute-start.2 = (bf16[64,768]{1,0:T(8,128)(2,1)S(1)}, bf16[64,768]{1,0:T(8,128)(2,1)S(1)}, u32[]{:S(2)}, u32[]{:S(2)}) collective-permute-start(bf16[64,768]{1,0:T(8,128)(2,1)S(1)} %get-tuple-element.321), channel_id=1, source_target_pairs={{4,0},{8,4},{12,8},{16,12},{20,16},{24,20},{28,24},{32,28},{36,32}... | collective-permute-start | bytes 294920 | tf_op jit(solution)/shard_map/while/body/eval_jaxpr/ppermute | solution.py:16
  200.7 8.0 %collective-permute-start.3 = (bf16[64,768]{1,0:T(8,128)(2,1)S(1)}, bf16[64,768]{1,0:T(8,128)(2,1)S(1)}, u32[]{:S(2)}, u32[]{:S(2)}) collective-permute-start(bf16[64,768]{1,0:T(8,128)(2,1)S(1)} %get-tuple-element.319), channel_id=1, source_target_pairs={{0,4},{4,8},{8,12},{12,16},{16,20},{20,24},{24,28},{28,32},{32,36}... | collective-permute-start | bytes 294920 | tf_op jit(solution)/shard_map/while/body/eval_jaxpr/ppermute | solution.py:16
  209.5 12.0 %collective-permute-start = (s32[64]{0:T(128)}, s32[64]{0:T(128)S(1)}, u32[]{:S(2)}, u32[]{:S(2)}) collective-permute-start(s32[64]{0:T(128)} %get-tuple-element.320), channel_id=1, source_target_pairs={{0,4},{4,8},{8,12},{12,16},{16,20},{20,24},{24,28},{28,32},{32,36}... | collective-permute-start | bytes 776 | tf_op jit(solution)/shard_map/while/body/eval_jaxpr/ppermute | solution.py:16
  211.4 10.1 %collective-permute-start.1 = (s32[64]{0:T(128)}, s32[64]{0:T(128)S(1)}, u32[]{:S(2)}, u32[]{:S(2)}) collective-permute-start(s32[64]{0:T(128)} %get-tuple-element.322), channel_id=1, source_target_pairs={{4,0},{8,4},{12,8},{16,12},{20,16},{24,20},{28,24},{32,28},{36,32}... | collective-permute-start | bytes 776 | tf_op jit(solution)/shard_map/while/body/eval_jaxpr/ppermute | solution.py:16
  217.2 5.5 %collective-permute-start.2 = (bf16[64,768]{1,0:T(8,128)(2,1)S(1)}, bf16[64,768]{1,0:T(8,128)(2,1)S(1)}, u32[]{:S(2)}, u32[]{:S(2)}) collective-permute-start(bf16[64,768]{1,0:T(8,128)(2,1)S(1)} %get-tuple-element.321), channel_id=1, source_target_pairs={{4,0},{8,4},{12,8},{16,12},{20,16},{24,20},{28,24},{32,28},{36,32}... | collective-permute-start | bytes 294920 | tf_op jit(solution)/shard_map/while/body/eval_jaxpr/ppermute | solution.py:16
  219.1 8.0 %collective-permute-start.3 = (bf16[64,768]{1,0:T(8,128)(2,1)S(1)}, bf16[64,768]{1,0:T(8,128)(2,1)S(1)}, u32[]{:S(2)}, u32[]{:S(2)}) collective-permute-start(bf16[64,768]{1,0:T(8,128)(2,1)S(1)} %get-tuple-element.319), channel_id=1, source_target_pairs={{0,4},{4,8},{8,12},{12,16},{16,20},{20,24},{24,28},{28,32},{32,36}... | collective-permute-start | bytes 294920 | tf_op jit(solution)/shard_map/while/body/eval_jaxpr/ppermute | solution.py:16
  228.0 12.0 %collective-permute-start = (s32[64]{0:T(128)}, s32[64]{0:T(128)S(1)}, u32[]{:S(2)}, u32[]{:S(2)}) collective-permute-start(s32[64]{0:T(128)} %get-tuple-element.320), channel_id=1, source_target_pairs={{0,4},{4,8},{8,12},{12,16},{16,20},{20,24},{24,28},{28,32},{32,36}... | collective-permute-start | bytes 776 | tf_op jit(solution)/shard_map/while/body/eval_jaxpr/ppermute | solution.py:16
  229.9 10.1 %collective-permute-start.1 = (s32[64]{0:T(128)}, s32[64]{0:T(128)S(1)}, u32[]{:S(2)}, u32[]{:S(2)}) collective-permute-start(s32[64]{0:T(128)} %get-tuple-element.322), channel_id=1, source_target_pairs={{4,0},{8,4},{12,8},{16,12},{20,16},{24,20},{28,24},{32,28},{36,32}... | collective-permute-start | bytes 776 | tf_op jit(solution)/shard_map/while/body/eval_jaxpr/ppermute | solution.py:16
  235.7 5.5 %collective-permute-start.2 = (bf16[64,768]{1,0:T(8,128)(2,1)S(1)}, bf16[64,768]{1,0:T(8,128)(2,1)S(1)}, u32[]{:S(2)}, u32[]{:S(2)}) collective-permute-start(bf16[64,768]{1,0:T(8,128)(2,1)S(1)} %get-tuple-element.321), channel_id=1, source_target_pairs={{4,0},{8,4},{12,8},{16,12},{20,16},{24,20},{28,24},{32,28},{36,32}... | collective-permute-start | bytes 294920 | tf_op jit(solution)/shard_map/while/body/eval_jaxpr/ppermute | solution.py:16
  237.6 8.0 %collective-permute-start.3 = (bf16[64,768]{1,0:T(8,128)(2,1)S(1)}, bf16[64,768]{1,0:T(8,128)(2,1)S(1)}, u32[]{:S(2)}, u32[]{:S(2)}) collective-permute-start(bf16[64,768]{1,0:T(8,128)(2,1)S(1)} %get-tuple-element.319), channel_id=1, source_target_pairs={{0,4},{4,8},{8,12},{12,16},{16,20},{20,24},{24,28},{28,32},{32,36}... | collective-permute-start | bytes 294920 | tf_op jit(solution)/shard_map/while/body/eval_jaxpr/ppermute | solution.py:16
  246.4 12.0 %collective-permute-start = (s32[64]{0:T(128)}, s32[64]{0:T(128)S(1)}, u32[]{:S(2)}, u32[]{:S(2)}) collective-permute-start(s32[64]{0:T(128)} %get-tuple-element.320), channel_id=1, source_target_pairs={{0,4},{4,8},{8,12},{12,16},{16,20},{20,24},{24,28},{28,32},{32,36}... | collective-permute-start | bytes 776 | tf_op jit(solution)/shard_map/while/body/eval_jaxpr/ppermute | solution.py:16
  248.4 10.1 %collective-permute-start.1 = (s32[64]{0:T(128)}, s32[64]{0:T(128)S(1)}, u32[]{:S(2)}, u32[]{:S(2)}) collective-permute-start(s32[64]{0:T(128)} %get-tuple-element.322), channel_id=1, source_target_pairs={{4,0},{8,4},{12,8},{16,12},{20,16},{24,20},{28,24},{32,28},{36,32}... | collective-permute-start | bytes 776 | tf_op jit(solution)/shard_map/while/body/eval_jaxpr/ppermute | solution.py:16
  254.1 5.5 %collective-permute-start.2 = (bf16[64,768]{1,0:T(8,128)(2,1)S(1)}, bf16[64,768]{1,0:T(8,128)(2,1)S(1)}, u32[]{:S(2)}, u32[]{:S(2)}) collective-permute-start(bf16[64,768]{1,0:T(8,128)(2,1)S(1)} %get-tuple-element.321), channel_id=1, source_target_pairs={{4,0},{8,4},{12,8},{16,12},{20,16},{24,20},{28,24},{32,28},{36,32}... | collective-permute-start | bytes 294920 | tf_op jit(solution)/shard_map/while/body/eval_jaxpr/ppermute | solution.py:16
  256.0 8.0 %collective-permute-start.3 = (bf16[64,768]{1,0:T(8,128)(2,1)S(1)}, bf16[64,768]{1,0:T(8,128)(2,1)S(1)}, u32[]{:S(2)}, u32[]{:S(2)}) collective-permute-start(bf16[64,768]{1,0:T(8,128)(2,1)S(1)} %get-tuple-element.319), channel_id=1, source_target_pairs={{0,4},{4,8},{8,12},{12,16},{16,20},{20,24},{24,28},{28,32},{32,36}... | collective-permute-start | bytes 294920 | tf_op jit(solution)/shard_map/while/body/eval_jaxpr/ppermute | solution.py:16
  266.4 35.1 %copy-start.1 = (bf16[64,768]{1,0:T(8,128)(2,1)S(1)}, bf16[64,768]{1,0:T(8,128)(2,1)}, u32[]{:S(2)}) copy-start(bf16[64,768]{1,0:T(8,128)(2,1)} %param.10) | copy-start | bytes 294916
  266.4 35.1 %slice-start = ((bf16[1,4,3,3072]{3,1,2,0:T(4,128)(2,1)}), bf16[1,4,1,3072]{3,1,2,0:T(4,128)(2,1)S(1)}, s32[]{:S(2)}) async-start(bf16[1,4,3,3072]{3,1,2,0:T(4,128)(2,1)} %param.12), calls=%async_computation.4 | async-start | bytes 49152 | tf_op jit(solution)/shard_map/slice | solution.py:50
  266.4 35.1 %copy-start.2 = (s32[64]{0:T(128)S(1)}, s32[64]{0:T(128)}, u32[]{:S(2)}) copy-start(s32[64]{0:T(128)} %param.11) | copy-start | bytes 772
  302.6 4.2 %collective-permute-start.4 = (bf16[64,384]{1,0:T(8,128)(2,1)S(1)}, bf16[64,384]{1,0:T(8,128)(2,1)S(1)}, u32[]{:S(2)}, u32[]{:S(2)}) collective-permute-start(bf16[64,384]{1,0:T(8,128)(2,1)S(1)} %constant_dynamic-slice_fusion), channel_id=1, source_target_pairs={{0,128},{128,0},{1,129},{129,1},{2,130},{130,2},{3,131},{131,3},{4... | collective-permute-start | bytes 147464 | tf_op jit(solution)/shard_map/ppermute | solution.py:26
Sparse Core Ops, SparseCore 0:
  9.9 64.4 all-gather.2
  76.9 61.5 all-gather.4
  278.4 22.9 reduce-scatter.1
where the time goes:
time: 316 us; the launch traced here: 314 us
  starting transfers between devices  145 us (46%)
  waiting for transfers between devices  84.4 us (27%)
  matrix products  29.8 us (9%)
  blocking collectives  19 us (6%)
  local copies, waits for them, and re-layouts  15.8 us (5%)
  between operations  13.3 us (4%)
  other arithmetic  5.61 us (2%)
    ppermute x48, starting transfers between devices, shifted(): return lax.ppermute(value, axis, pairs)  144 us
    ppermute x48, waiting for transfers between devices, shifted(): return lax.ppermute(value, axis, pairs)  56.2 us
    reduce_scatter x1, waiting for transfers between devices, on_device(): lax.psum_scatter(partial_term.astype(jnp.bfloat16), 'tp', scatter_dimensi...  23.1 us
    all_gather x1, blocking collectives, on_device(): full = lax.all_gather(hidden, 'tp', axis=1, tiled=True)  19 us
    while x84, local copies, waits for them, and re-layouts  13 us
    dot_general x1, matrix products, on_device(): lax.dot_general(mlp_act, lax.all_gather(w_mlp_back, 'seq', axis=0, tiled=...  11.9 us
  transfers between devices with their start and end apart: 52, of which 16 were waited for; matrix products, arithmetic and copies ran while one was open for 12% of the time, Pallas kernels for 0%

commit v1 on v0

--- a/solution.py
+++ b/solution.py
@@ -8,12 +8,6 @@
 
 
 guidance = 3.5
-
-
-def shifted(value, axis, by):
-    devices = lax.axis_size(axis)
-    pairs = [(i, i + by) for i in range(devices) if 0 <= i + by < devices]
-    return lax.ppermute(value, axis, pairs)
 
 
 def from_partner(block, axis, apart):
@@ -37,7 +31,6 @@
     heads_here = group // HEAD
     requests = modulation.shape[1]
     tp_index = lax.axis_index("tp")
-    reach = min(lax.axis_size("seq") - 1, 12)
     full = lax.all_gather(hidden, "tp", axis=1, tiled=True)
     xf = full.astype(jnp.float32)
     centred = xf - jnp.mean(xf, axis=-1, keepdims=True)
@@ -65,51 +58,21 @@
     packed = jnp.concatenate([key_rows.reshape(rows, group), value_rows], axis=1)
     seg_plus = seg_ids + 1
 
-    def attend_block(state, kv_block, seg_block):
-        peak, total, summed = state
-        count = kv_block.shape[0]
-        keys = kv_block[:, :group].reshape(count, heads_here, HEAD)
-        values = kv_block[:, group:].reshape(count, heads_here, HEAD)
-        score = jnp.einsum(
-            "qhe,khe->hqk", query, keys, preferred_element_type=jnp.float32
-        ) * HEAD ** (-0.5)
-        score = jnp.where((seg_plus[:, None] == seg_block[None, :])[None], score, -1e30)
-        new_peak = jnp.maximum(peak, jnp.max(score, axis=-1))
-        factor = jnp.exp(peak - new_peak)
-        weight = jnp.exp(score - new_peak[:, :, None])
-        total = total * factor + jnp.sum(weight, axis=-1)
-        summed = summed * factor[:, :, None] + jnp.einsum(
-            "hqk,khe->hqe", weight.astype(jnp.bfloat16), values, preferred_element_type=jnp.float32
-        )
-        return (new_peak, total, summed)
-
-    def absorb(state, kv_piece, seg_piece):
-        blocks = kv_piece.shape[0] // rows
-
-        def step(index, carry):
-            return attend_block(carry, kv_piece, seg_piece)
-
-        return lax.fori_loop(0, blocks, step, state)
-
-    start_state = (
-        jnp.full((heads_here, rows), -1e30, jnp.float32),
-        jnp.zeros((heads_here, rows), jnp.float32),
-        jnp.zeros((heads_here, rows, HEAD), jnp.float32),
+    keys_all = lax.all_gather(packed, "seq", axis=0, tiled=True)
+    seg_all = lax.all_gather(seg_plus, "seq", axis=0, tiled=True)
+    count = keys_all.shape[0]
+    keys = keys_all[:, :group].reshape(count, heads_here, HEAD)
+    values = keys_all[:, group:].reshape(count, heads_here, HEAD)
+    score = jnp.einsum(
+        "qhe,khe->hqk", query, keys, preferred_element_type=jnp.float32
+    ) * HEAD ** (-0.5)
+    score = jnp.where((seg_plus[:, None] == seg_all[None, :])[None], score, -1e30)
+    peak = jnp.max(score, axis=-1, keepdims=True)
+    weight = jnp.exp(score - peak)
+    total = jnp.sum(weight, axis=-1)
+    summed = jnp.einsum(
+        "hqk,khe->hqe", weight.astype(jnp.bfloat16), values, preferred_element_type=jnp.float32
     )
-    first = absorb(start_state, packed, seg_plus)
-
-    def turn(index, carry):
-        state_now, lower, upper = carry
-        lower = shifted((lower[0], lower[1]), "seq", 1)
-        upper = shifted((upper[0], upper[1]), "seq", -1)
-        state_now = absorb(state_now, lower[0], lower[1])
-        state_now = absorb(state_now, upper[0], upper[1])
-        return (state_now, lower, upper)
-
-    state, unused_low, unused_high = lax.fori_loop(
-        0, reach, turn, (first, (packed, seg_plus), (packed, seg_plus))
-    )
-    peak, total, summed = state
     attended = (summed / total[:, :, None]).astype(jnp.bfloat16)
     attended = jnp.transpose(attended, (1, 0, 2)).reshape(rows, group)
     mlp_term = lax.dot_general(

time: 316 us -> 260 us (0.82)
  starting transfers between devices: 145 us -> 0.7 us
  waiting for transfers between devices: 84.4 us -> 173 us
  blocking collectives: 19 us -> 34 us
  matrix products: 29.8 us -> 21.4 us
  local copies, waits for them, and re-layouts: 15.8 us -> 12.6 us
    ppermute x48 -> x0, starting transfers between devices: 144 us -> none  [shifted(): return lax.ppermute(value, axis, pairs)]
    all_gather x1, waiting for transfers between devices: 0.02 us -> 62.7 us  [on_device(): lax.all_gather(w_mlp_back, 'seq', axis=0, tiled=True)]
    ppermute x48 -> x0, waiting for transfers between devices: 56.2 us -> none  [shifted(): return lax.ppermute(value, axis, pairs)]
    all_gather x1, waiting for transfers between devices: 0.01 us -> 49.3 us  [on_device(): lax.all_gather(w_mlp_in, 'seq', axis=0, tiled=True)]
    all_gather x0 -> x1, waiting for transfers between devices: none -> 30.4 us  [on_device(): keys_all = lax.all_gather(packed, 'seq', axis=0, tiled=True)]
    unnamed x0 -> x1, blocking collectives: none -> 14.9 us
    while x84 -> x0, local copies, waits for them, and re-layouts: 13 us -> none
    slice x2 -> x3, local copies, waits for them, and re-layouts: 0.02 us -> 9.15 us  [the longest x2 6.53 us: on_device(): keys = keys_all[:, :group].reshape(count, heads_here, HEAD)]
  transfers between devices with their start and end apart: 52 -> 5, of which waited for: 16 -> 5; matrix products, arithmetic and copies ran while one was open for 12% -> 6% of each run, Pallas kernels for 0% -> 0%
where the time goes in v1:
time: 260 us; the launch traced here: 259 us
  waiting for transfers between devices  173 us (67%)
  blocking collectives  34 us (13%)
  matrix products  21.4 us (8%)
  between operations  14 us (5%)
  local copies, waits for them, and re-layouts  12.6 us (5%)
  other arithmetic  3.08 us (1%)
    all_gather x1, waiting for transfers between devices, on_device(): lax.all_gather(w_mlp_back, 'seq', axis=0, tiled=True)  62.7 us
    all_gather x1, waiting for transfers between devices, on_device(): lax.all_gather(w_mlp_in, 'seq', axis=0, tiled=True)  49.3 us
    all_gather x1, waiting for transfers between devices, on_device(): keys_all = lax.all_gather(packed, 'seq', axis=0, tiled=True)  30.4 us
    reduce_scatter x1, waiting for transfers between devices, on_device(): lax.psum_scatter(partial_term.astype(jnp.bfloat16), 'tp', scatter_dimensi...  25.8 us
    all_gather x1, blocking collectives, on_device(): full = lax.all_gather(hidden, 'tp', axis=1, tiled=True)  19.1 us
    unnamed x1, blocking collectives  14.9 us
    dot_general x1, matrix products, on_device(): lax.dot_general(mlp_act, lax.all_gather(w_mlp_back, 'seq', axis=0, tiled=...  11.7 us
    slice x2, local copies, waits for them, and re-layouts, on_device(): keys = keys_all[:, :group].reshape(count, heads_here, HEAD)  6.53 us
  transfers between devices with their start and end apart: 5, of which 5 were waited for; matrix products, arithmetic and copies ran while one was open for 6% of the time, Pallas kernels for 0%

profile of v1, /device:TPU:4, one launch (start us, length us, event | category | flops | bytes accessed | tf_op | source)
XLA Modules:
  0.0 259.2 jit_solution(889151841724916340)
XLA Ops:
  6.5 0.0 copy-start
  6.5 0.0 all-gather.4.cloned.1.call-start
  6.5 19.1 %all_gather.16 = bf16[64,3072]{1,0:T(8,128)(2,1)S(1)} all-gather(bf16[64,768]{1,0:T(8,128)(2,1)} %param.8), channel_id=1, replica_groups=mesh['guide'=2,'seq'=32,'tp'=4] {'tp'}, dimensions={1}, use_global_device_ids=true | all-gather | bytes 491520 | tf_op jit(solution)/shard_map/all_gather | solution.py:34
  25.6 0.2 convert_reduce_fusion
  25.8 0.3 fusion.11
  26.1 0.8 slice.35
  26.9 1.1 fusion.42
  28.0 0.2 fusion.14
  28.2 0.0 copy-start.3
  28.2 4.3 %fusion.25 = f32[64,3,384]{2,0,1:T(8,128)S(1)} fusion(bf16[3072,3,384]{2,0,1:T(8,128)(2,1)} %param.12, bf16[64,3072]{1,0:T(8,128)(2,1)S(1)} %fusion.14), kind=kOutput, calls=%fused_computation.33 | convolution fusion | flops 452984832 | bytes 7766016 | tf_op jit(solution)/shard_map/td,dck->tck/dot_general | solution.py:52
  32.5 0.0 copy-start.4
  32.5 0.0 copy-start.2
  32.6 0.1 reduce_sum.48
  32.8 0.0 copy-done.3
  32.8 0.1 mul.133
  33.0 0.7 pad_maximum_fusion
  33.7 0.0 all-gather.4.cloned.1.call-update
  33.7 0.0 all-gather.6.cloned.1.call-start
  33.7 0.7 all-gather.6.cloned.1.call-update
  34.4 0.0 all-gather.8.cloned.1.call-start
  34.5 0.7 all-gather.8.cloned.1.call-update
  35.2 0.0 reduce-scatter.2.cloned.1.call-start
  35.3 0.0 copy-done.4
  35.3 0.6 dynamic-slice.1
  36.5 0.0 copy-done.2
  36.5 0.1 broadcast_add_fusion
  36.7 14.9 %all-reduce = s32[2048]{0:T(1024)S(1)} all-reduce(s32[2048]{0:T(1024)S(1)} %get-tuple-element.12), channel_id=1, replica_groups=mesh['guide'=2,'seq'=32,'tp'=4] {'seq'}, use_global_device_ids=true, to_apply=%add | all-reduce | flops 2048 | bytes 16384
  51.6 0.1 multiply_reduce_fusion
  51.8 0.1 multiply_convert_fusion
  51.9 0.1 broadcast_compare_fusion
  52.1 30.4 %all-gather.4.cloned.1.call-done = bf16[2048,768]{1,0:T(8,128)(2,1)} async-done(((bf16[64,768]{1,0:T(8,128)(2,1)}), bf16[2048,768]{1,0:T(8,128)(2,1)}) %all-gather.4.cloned.1.call-update) | async-done | bytes 3145744 | tf_op jit(solution)/shard_map/all_gather | solution.py:61
  82.5 3.9 %fusion.53 = (bf16[2048,384]{1,0:T(8,128)(2,1)}, bf16[2048,384]{1,0:T(8,128)(2,1)}) fusion(bf16[2048,768]{1,0:T(8,128)(2,1)} %all-gather.4.cloned.1.call-done), kind=kLoop, calls=%fused_computation.79 | loop fusion | bytes 6291456 | tf_op jit(solution)/shard_map/slice | solution.py:64
  86.4 2.6 %copy.31 = bf16[2048,384]{0,1:T(8,128)(2,1)} copy(bf16[2048,384]{1,0:T(8,128)(2,1)} %get-tuple-element.5) | data formatting | bytes 3145728 | tf_op jit(solution)/shard_map/slice | solution.py:64
  89.0 2.6 %copy.34 = bf16[2048,384]{0,1:T(8,128)(2,1)} copy(bf16[2048,384]{1,0:T(8,128)(2,1)} %get-tuple-element.6) | data formatting | bytes 3145728 | tf_op jit(solution)/shard_map/slice | solution.py:65
  91.7 2.0 fusion.55
  93.7 0.0 copy-start.1
  93.7 0.4 fusion.2
  94.0 1.0 copy-done.1
  95.1 0.7 fusion.8
  95.8 0.0 copy-done
  95.8 0.5 fusion.38
  96.3 49.3 %all-gather.6.cloned.1.call-done = bf16[3072,1536]{1,0:T(8,128)(2,1)} async-done(((bf16[96,1536]{1,0:T(8,128)(2,1)}), bf16[3072,1536]{1,0:T(8,128)(2,1)}) %all-gather.6.cloned.1.call-update) | async-done | bytes 9437200 | tf_op jit(solution)/shard_map/all_gather | solution.py:48
  145.7 62.7 %all-gather.8.cloned.1.call-done = bf16[3072,1536]{1,0:T(8,128)(2,1)} async-done(((bf16[96,1536]{1,0:T(8,128)(2,1)}), bf16[3072,1536]{1,0:T(8,128)(2,1)}) %all-gather.8.cloned.1.call-update) | async-done | bytes 9437200 | tf_op jit(solution)/shard_map/all_gather | solution.py:80
  208.4 11.7 %fusion = bf16[64,3072]{1,0:T(8,128)(2,1)} fusion(f32[64,3072]{1,0:T(8,128)S(1)} %fusion.38, bf16[3072,1536]{1,0:T(8,128)(2,1)} %all-gather.8.cloned.1.call-done, bf16[64,3072]{1,0:T(8,128)(2,1)S(1)} %fusion.14, bf16[3072,1536]{1,0:T(8,128)(2,1)} %all-gather.6.cloned.1.call-done), kind=kOutput, calls=%fused_computation.1 | convolution fusion | flops 1209237504 | bytes 20447232 | tf_op jit(solution)/shard_map/dot_general | solution.py:78
  220.0 0.0 reduce-scatter.2.cloned.1.call-update
  220.1 0.8 slice.34
  220.8 25.8 %reduce-scatter.2.cloned.1.call-done = bf16[64,768]{1,0:T(8,128)(2,1)} async-done(((bf16[64,3072]{1,0:T(8,128)(2,1)}), bf16[64,768]{1,0:T(8,128)(2,1)}) %reduce-scatter.2.cloned.1.call-update) | async-done | bytes 98320 | tf_op jit(solution)/shard_map/reduce_scatter | solution.py:85
  246.6 1.2 fusion.5
  247.8 0.6 collective-permute-start
  248.4 3.6 %collective-permute-done = bf16[64,384]{1,0:T(8,128)(2,1)S(1)} collective-permute-done((bf16[64,384]{1,0:T(8,128)(2,1)S(1)}, bf16[64,384]{1,0:T(8,128)(2,1)S(1)}, u32[]{:S(2)}, u32[]{:S(2)}) %collective-permute-start) | collective-permute-done | bytes 49184 | tf_op jit(solution)/shard_map/ppermute | solution.py:20
  252.0 0.6 fusion.37
  (13 shorter events, 0.2 us)
Async XLA Ops:
  6.5 89.3 %copy-start = (bf16[384,3072]{1,0:T(8,128)(2,1)S(1)}, bf16[384,3072]{1,0:T(8,128)(2,1)}, u32[]{:S(2)}) copy-start(bf16[384,3072]{1,0:T(8,128)(2,1)} %param.14) | copy-start | bytes 7077892
  6.5 76.0 %all-gather.4.cloned.1.call-start = ((), (), s32[]{:S(2)}) async-start(), calls=%async_computation.1 | async-start | bytes 3244032 | tf_op jit(solution)/shard_map/all_gather | solution.py:61
  28.2 4.6 %copy-start.3 = (f32[2,128]{1,0:T(2,128)S(1)}, f32[2,128]{1,0:T(2,128)}, u32[]{:S(2)}) copy-start(f32[2,128]{1,0:T(2,128)} %param.11) | copy-start | bytes 3076
  32.5 2.7 %copy-start.4 = (u32[256]{0:T(256)S(1)}, u32[256]{0:T(256)}, u32[]{:S(2)}) copy-start(u32[256]{0:T(256)} %constant.55) | copy-start | bytes 3076
  32.5 4.0 %copy-start.2 = (s32[64]{0:T(128)S(1)}, s32[64]{0:T(128)}, u32[]{:S(2)}) copy-start(s32[64]{0:T(128)} %param.9) | copy-start | bytes 772
  33.7 112.0 %all-gather.6.cloned.1.call-start = ((), (), s32[]{:S(2)}) async-start(), calls=%async_computation.2 | async-start | bytes 9732096 | tf_op jit(solution)/shard_map/all_gather | solution.py:48
  34.4 173.9 %all-gather.8.cloned.1.call-start = ((), (), s32[]{:S(2)}) async-start(), calls=%async_computation.3 | async-start | bytes 9732096 | tf_op jit(solution)/shard_map/all_gather | solution.py:80
  35.2 211.4 %reduce-scatter.2.cloned.1.call-start = ((), (), s32[]{:S(2)}) async-start(), calls=%async_computation.4 | async-start | bytes 491520 | tf_op jit(solution)/shard_map/reduce_scatter | solution.py:85
  93.7 1.4 copy-start.1
  247.8 4.2 %collective-permute-start = (bf16[64,384]{1,0:T(8,128)(2,1)S(1)}, bf16[64,384]{1,0:T(8,128)(2,1)S(1)}, u32[]{:S(2)}, u32[]{:S(2)}) collective-permute-start(bf16[64,384]{1,0:T(8,128)(2,1)S(1)} %constant_dynamic-slice_fusion), channel_id=1, source_target_pairs={{0,128},{128,0},{1,129},{129,1},{2,130},{130,2},{3,131},{131,3},{4... | collective-permute-start | bytes 147464 | tf_op jit(solution)/shard_map/ppermute | solution.py:20
Sparse Core Ops, SparseCore 0:
  33.8 48.6 all-gather.3
  85.0 60.5 all-gather.5
  148.2 60.0 all-gather.7
  220.2 26.3 reduce-scatter.1

commit v2 on v1

v2 whole, which is shorter than its diff:
```python
import jax
import jax.numpy as jnp
from jax import lax
from jax.experimental import pallas as pl
from jax.experimental.pallas import tpu as pltpu
from jax.sharding import PartitionSpec as P

D = 3072
HEAD = 128
ROWS = 64
WIDE = 768
GROUP = 384
SLAB = 96
HEADS_HERE = 3
REQUESTS = 4
KV = 2 * GROUP + HEAD
GUIDANCE = 3.5
COPIES = 132
LOCALS = 10

F32 = jnp.float32
BF16 = jnp.bfloat16


def dot(a, b):
    return jnp.dot(a, b, preferred_element_type=F32)


def dot_t(a, b):
    return lax.dot_general(a, b, (((1,), (1,)), ((), ())), preferred_element_type=F32)


class Links:
    def __init__(self, send_sems, recv_sems):
        self.send_sems, self.recv_sems = send_sems, recv_sems
        self.used = 0
        self.sent = []

    def copy(self, src, dst, device):
        i = self.used
        self.used += 1
        made = pltpu.make_async_remote_copy(
            src_ref=src,
            dst_ref=dst,
            send_sem=self.send_sems.at[i],
            recv_sem=self.recv_sems.at[i],
            device_id=device,
            device_id_type=pl.DeviceIdType.MESH,
        )
        self.sent.append(made)
        return made

    def drain(self):
        for made in self.sent:
            made.wait_send()


class RingGather:
    def __init__(self, links, right, left, own, at_right, at_left, from_left, from_right, on_right, on_left):
        self.first = [
            links.copy(own(0), at_right(0), right),
            links.copy(own(1), at_left(1), left),
            links.copy(own(1), at_right(1), right),
            links.copy(own(0), at_left(0), left),
        ]
        self.onward = [
            links.copy(from_left(0), on_right(0), right),
            links.copy(from_right(1), on_left(1), left),
        ]

    def start(self):
        for made in self.first:
            made.start()

    def forward(self):
        self.first[0].wait_recv()
        self.onward[0].start()
        self.first[1].wait_recv()
        self.onward[1].start()

    def finish(self):
        self.first[2].wait_recv()
        self.first[3].wait_recv()
        self.onward[0].wait_recv()
        self.onward[1].wait_recv()


def body(
    hidden, seg, modulation, qk_gain, w_qkv, w_in, w_out, w_back,
    result,
    hid, xm, win, wback, relay, kv, wqkv_v, wout_v, mod_v, gain_v, seg_v, q_v, act_v,
    pacc, rs_out, rs_opp, rs_left, rs_right, z_out, z_in, own_out, other_out,
    send_sems, recv_sems, local_sems,
):
    g = lax.axis_index("guide")
    s = lax.axis_index("seq")
    t = lax.axis_index("tp")
    x, y, c = s // 8, (s % 8) // 2, s % 2
    yr, yl, yo = (y + 1) % 4, (y + 3) % 4, (y + 2) % 4

    def at_seq(xx, yy, cc):
        return {"seq": xx * 8 + yy * 2 + cc}

    x_right, x_left = at_seq((x + 1) % 4, y, c), at_seq((x + 3) % 4, y, c)
    y_right, y_left = at_seq(x, yr, c), at_seq(x, yl, c)
    mate = at_seq(x, y, 1 - c)
    t_right, t_left, t_far = {"tp": (t + 1) % 4}, {"tp": (t + 3) % 4}, {"tp": (t + 2) % 4}
    partner = {"guide": 1 - g}

    barrier = pltpu.get_barrier_semaphore()
    everyone = (x_right, x_left, y_right, y_left, mate, t_right, t_left, t_far, partner)
    for device in everyone:
        pl.semaphore_signal(barrier, inc=1, device_id=device, device_id_type=pl.DeviceIdType.MESH)

    pairs = [
        (hidden, hid.at[0]),
        (seg, seg_v),
        (modulation, mod_v),
        (qk_gain, gain_v),
        (w_qkv.at[1], wqkv_v.at[1]),
        (w_qkv.at[2], wqkv_v.at[2]),
        (w_qkv.at[0], wqkv_v.at[0]),
        (w_out, wout_v),
        (w_in.at[:, pl.ds(pl.multiple_of(x * GROUP, GROUP), GROUP)], win.at[0, y, c]),
        (w_back.at[:, pl.ds(pl.multiple_of(x * GROUP, GROUP), GROUP)], wback.at[0, y, c]),
    ]
    local = [pltpu.make_async_copy(a, b, local_sems.at[i]) for i, (a, b) in enumerate(pairs)]
    for made in local:
        made.start()
    pl.semaphore_wait(barrier, len(everyone))

    links = Links(send_sems, recv_sems)

    half32 = lambda h: pl.ds(h * 32, 32)
    half48 = lambda h: pl.ds(h * 48, 48)

    def x_gather(buffer, own=None):
        spot = lambda d: (lambda h: buffer.at[d, half32(h)])
        return RingGather(
            links, x_right, x_left, own or spot(0), spot(3), spot(1), spot(3), spot(1), spot(2), spot(2)
        )

    tp_spot = lambda d: (lambda h: hid.at[d, half32(h)])
    hid_gather = RingGather(
        links, t_right, t_left, lambda h: hidden.at[half32(h)], tp_spot(3), tp_spot(1), tp_spot(3), tp_spot(1),
        tp_spot(2), tp_spot(2),
    )

    def y_gather(buffer, low, high, half, own=None):
        spot = lambda yy: (lambda h: buffer.at[low:high, yy, c, half(h)])
        return RingGather(
            links, y_right, y_left, own or spot(y), spot(y), spot(y), spot(yl), spot(yr), spot(yl), spot(yr)
        )

    def columns(weight, dx, h=None):
        cols = pl.ds(pl.multiple_of(((x + dx) % 4) * GROUP, GROUP), GROUP)
        return weight.at[:, cols] if h is None else weight.at[half48(h), cols]

    class Weights:
        def __init__(self, source, buffer, which):
            self.to_right = links.copy(columns(source, 1), buffer.at[3, y, c], x_right)
            self.to_left = links.copy(columns(source, 3), buffer.at[1, y, c], x_left)
            self.far = [
                links.copy(columns(source, 2, 0), relay.at[which, 0], x_right),
                links.copy(columns(source, 2, 1), relay.at[which, 1], x_left),
            ]
            self.onward = [
                links.copy(relay.at[which, 0], buffer.at[2, y, c, half48(0)], x_right),
                links.copy(relay.at[which, 1], buffer.at[2, y, c, half48(1)], x_left),
            ]
            self.near = y_gather(buffer, 0, 1, half48)
            self.rest = y_gather(buffer, 1, 4, half48)
            self.over = [
                links.copy(buffer.at[0:1, :, c], buffer.at[0:1, :, c], mate),
                links.copy(buffer.at[1:4, :, c], buffer.at[1:4, :, c], mate),
            ]

        def start(self):
            for made in self.far:
                made.start()
            self.to_right.start()
            self.to_left.start()

        def relay(self):
            for arrived, onward in zip(self.far, self.onward):
                arrived.wait_recv()
                onward.start()

        def second(self):
            self.to_right.wait_recv()
            self.to_left.wait_recv()
            for made in self.onward:
                made.wait_recv()
            self.rest.start()

    weights_in = Weights(w_in, win, 0)
    weights_back = Weights(w_back, wback, 1)
    xm_gather = x_gather(xm)
    kv_x = RingGather(
        links, x_right, x_left, *[
            (lambda d: (lambda h: kv.at[d, y, c, half32(h)]))(d) for d in (0, 3, 1, 3, 1, 2, 2)
        ]
    )
    kv_near = y_gather(kv, 0, 1, half32)
    kv_rest = y_gather(kv, 1, 4, half32)
    kv_over = [
        links.copy(kv.at[0:1, :, c], kv.at[0:1, :, c], mate),
        links.copy(kv.at[1:4, :, c], kv.at[1:4, :, c], mate),
    ]

    hid_gather.start()
    weights_in.start()
    local[8].wait()
    weights_in.near.start()
    weights_back.start()
    local[9].wait()
    weights_back.near.start()

    for made in local[:4]:
        made.wait()
    hid_gather.forward()
    weights_in.relay()
    weights_in.near.forward()
    weights_in.second()
    hid_gather.finish()

    seg_row = jnp.broadcast_to(seg_v[...].astype(F32), (ROWS, ROWS))
    at_row = lax.broadcasted_iota(jnp.int32, (ROWS, ROWS), 0)
    at_col = lax.broadcasted_iota(jnp.int32, (ROWS, ROWS), 1)
    seg_col = jnp.sum(jnp.where(at_row == at_col, seg_row, 0.0), axis=-1, keepdims=True)

    def look_up(kind, offset):
        table = mod_v[kind, :, pl.ds(pl.multiple_of(offset, WIDE), WIDE)].astype(F32)
        found = jnp.broadcast_to(table[0:1], (ROWS, WIDE))
        for r in range(1, REQUESTS):
            found = jnp.where(seg_col == float(r), table[r : r + 1], found)
        return found

    total = sum(jnp.sum(hid[d].astype(F32), axis=-1, keepdims=True) for d in range(4))
    mean = total * (1.0 / D)
    squares = jnp.zeros((ROWS, 1), F32)
    for d in range(4):
        centred = hid[d].astype(F32) - mean
        squares += jnp.sum(centred * centred, axis=-1, keepdims=True)
    scale_rows = lax.rsqrt(squares * (1.0 / D) + 1e-06)
    for d in range(4):
        offset = ((t + d) % 4) * WIDE
        normed = (hid[d].astype(F32) - mean) * scale_rows
        xm[0, :, pl.ds(pl.multiple_of(offset, WIDE), WIDE)] = (
            normed * (1.0 + look_up(1, offset)) + look_up(0, offset)
        ).astype(BF16)
    xm_gather.start()

    weights_back.relay()
    weights_back.near.forward()
    weights_back.second()

    def head_norm(values, gain):
        return values * lax.rsqrt(jnp.mean(values * values, axis=-1, keepdims=True) + 1e-06) * gain

    rows_own = xm[0]
    local[4].wait()
    keys = dot(rows_own, wqkv_v[1])
    for h in range(HEADS_HERE):
        cols = slice(h * HEAD, (h + 1) * HEAD)
        kv[0, y, c, :, cols] = head_norm(keys[:, cols], gain_v[1:2, :]).astype(BF16)
    local[5].wait()
    kv[0, y, c, :, GROUP : 2 * GROUP] = dot(rows_own, wqkv_v[2]).astype(BF16)
    lane = lax.broadcasted_iota(jnp.int32, (ROWS, HEAD), 1).astype(F32)
    one_hot = jnp.where(seg_col == lane, 1.0, 0.0).astype(BF16)
    kv[0, y, c, :, 2 * GROUP :] = one_hot
    kv_x.start()
    kv_near.start()

    weights_in.rest.forward()
    weights_in.near.finish()
    weights_in.over[0].start()

    local[6].wait()
    query = dot(rows_own, wqkv_v[0])
    for h in range(HEADS_HERE):
        cols = slice(h * HEAD, (h + 1) * HEAD)
        q_v[:, cols] = head_norm(query[:, cols], gain_v[0:1, :]).astype(BF16)

    weights_back.near.finish()
    weights_back.over[0].start()
    weights_back.rest.forward()
    weights_in.rest.finish()
    weights_in.over[1].start()
    xm_gather.forward()
    kv_x.forward()
    kv_near.forward()
    kv_x.finish()
    kv_rest.start()
    weights_back.rest.finish()
    weights_back.over[1].start()
    xm_gather.finish()
    for made in weights_in.over:
        made.wait_recv()

    pre = jnp.zeros((4 * ROWS, GROUP), F32)
    for d in range(4):
        cols = pl.ds(pl.multiple_of(((x + d) % 4) * WIDE, WIDE), WIDE)
        pre += dot(xm[:, :, cols].reshape(4 * ROWS, WIDE), win[d].reshape(WIDE, GROUP))
    act_v[...] = jax.nn.gelu(pre, approximate=True).astype(BF16)

    kv_near.finish()
    kv_over[0].start()
    for made in weights_back.over:
        made.wait_recv()

    low, high = slice(0, GROUP), slice(GROUP, WIDE)
    chunks = []
    for k, step in enumerate((2, 1, 3, 0)):
        e = (t + step) % 4
        part = dot_t(act_v[...], wback[(e - x + 4) % 4].reshape(WIDE, GROUP))
        pacc[k] = part.reshape(4, ROWS, WIDE)
        rs_out[k, 0] = part[2 * ROWS : 3 * ROWS, low].astype(BF16)
        rs_out[k, 1] = part[2 * ROWS : 3 * ROWS, high].astype(BF16)
        rs_out[k, 2] = part[ROWS : 2 * ROWS, high].astype(BF16)
        rs_out[k, 3] = part[3 * ROWS :, low].astype(BF16)
        first = [
            links.copy(rs_out.at[k, 0], rs_opp.at[k, 0], x_right),
            links.copy(rs_out.at[k, 1], rs_opp.at[k, 1], x_left),
            links.copy(rs_out.at[k, 2], rs_left.at[k, 1], x_right),
            links.copy(rs_out.at[k, 3], rs_right.at[k, 0], x_left),
        ]
        second = [
            links.copy(rs_out.at[k, 4], rs_left.at[k, 0], x_right),
            links.copy(rs_out.at[k, 5], rs_right.at[k, 1], x_left),
        ]
        chunks.append((first, second))
        for made in first:
            made.start()

    def merge(k):
        first, second = chunks[k]
        first[0].wait_recv()
        rs_out[k, 4] = (pacc[k, 1, :, low] + rs_opp[k, 0].astype(F32)).astype(BF16)
        second[0].start()
        first[1].wait_recv()
        rs_out[k, 5] = (pacc[k, 3, :, high] + rs_opp[k, 1].astype(F32)).astype(BF16)
        second[1].start()

    kv_rest.forward()
    merge(0)
    merge(1)
    kv_rest.finish()
    kv_over[1].start()
    merge(2)
    merge(3)
    for made in kv_over:
        made.wait_recv()

    everything = kv.reshape(32 * ROWS, KV)
    same = dot_t(one_hot, everything[:, 2 * GROUP :]) > 0.5
    attended = []
    for h in range(HEADS_HERE):
        k_cols = slice(h * HEAD, (h + 1) * HEAD)
        v_cols = slice(GROUP + h * HEAD, GROUP + (h + 1) * HEAD)
        score = dot_t(q_v[:, k_cols], everything[:, k_cols]) * HEAD ** (-0.5)
        score = jnp.where(same, score, -1e30)
        weight = jnp.exp(score - jnp.max(score, axis=-1, keepdims=True))
        summed = dot(weight.astype(BF16), everything[:, v_cols])
        attended.append((summed / jnp.sum(weight, axis=-1, keepdims=True)).astype(BF16))
    attended = jnp.concatenate(attended, axis=1)
    local[7].wait()

    branch = jnp.zeros((ROWS, WIDE), F32)
    sends = []
    for k, step in enumerate((2, 1, 3, 0)):
        e = (t + step) % 4
        term = dot(attended, wout_v[:, pl.ds(pl.multiple_of(e * WIDE, WIDE), WIDE)])
        first, second = chunks[k]
        first[2].wait_recv()
        first[3].wait_recv()
        second[0].wait_recv()
        second[1].wait_recv()
        mlp_low = pacc[k, 0, :, low] + rs_left[k, 0].astype(F32) + rs_right[k, 0].astype(F32)
        mlp_high = pacc[k, 0, :, high] + rs_left[k, 1].astype(F32) + rs_right[k, 1].astype(F32)
        term = (term + jnp.concatenate([mlp_low, mlp_high], axis=1)).astype(BF16)
        if k < 3:
            z_out[k] = term
            made = links.copy(z_out.at[k], z_in.at[k], (t_far, t_right, t_left)[k])
            made.start()
            sends.append(made)
        else:
            branch = term.astype(F32)
    gate = look_up(2, t * WIDE)
    for k, made in enumerate(sends):
        made.wait_recv()
        branch += z_in[k].astype(F32)
    own_out[...] = (hid[0].astype(F32) + gate * branch).astype(BF16)
    kept_cols = pl.ds(pl.multiple_of(g * GROUP, GROUP), GROUP)
    handed_cols = pl.ds(pl.multiple_of((1 - g) * GROUP, GROUP), GROUP)
    swap = links.copy(own_out.at[:, handed_cols], other_out, partner)
    swap.start()
    kept = own_out[:, kept_cols].astype(F32)
    swap.wait_recv()
    other = other_out[...].astype(F32)
    cond = jnp.where(g == 0, kept, other)
    uncond = jnp.where(g == 0, other, kept)
    result[...] = (uncond + GUIDANCE * (cond - uncond)).astype(BF16)
    links.drain()


def on_device(hidden, seg_ids, modulation, qk_gain, w_qkv, w_mlp_in, w_out, w_mlp_back):
    anywhere = pl.BlockSpec(memory_space=pl.ANY)
    guided = pl.pallas_call(
        body,
        out_shape=jax.ShapeDtypeStruct((ROWS, GROUP), BF16),
        in_specs=[anywhere] * 8,
        out_specs=pl.BlockSpec(memory_space=pltpu.VMEM),
        scratch_shapes=[
            pltpu.VMEM((4, ROWS, WIDE), BF16),
            pltpu.VMEM((4, ROWS, D), BF16),
            pltpu.VMEM((4, 4, 2, SLAB, GROUP), BF16),
            pltpu.VMEM((4, 4, 2, SLAB, GROUP), BF16),
            pltpu.VMEM((2, 2, SLAB // 2, GROUP), BF16),
            pltpu.VMEM((4, 4, 2, ROWS, KV), BF16),
            pltpu.VMEM((3, D, GROUP), BF16),
            pltpu.VMEM((GROUP, D), BF16),
            pltpu.VMEM((3, REQUESTS, D), BF16),
            pltpu.VMEM((2, HEAD), F32),
            pltpu.VMEM((1, ROWS), jnp.int32),
            pltpu.VMEM((ROWS, GROUP), BF16),
            pltpu.VMEM((4 * ROWS, GROUP), BF16),
            pltpu.VMEM((4, 4, ROWS, WIDE), F32),
            pltpu.VMEM((4, 6, ROWS, GROUP), BF16),
            pltpu.VMEM((4, 2, ROWS, GROUP), BF16),
            pltpu.VMEM((4, 2, ROWS, GROUP), BF16),
            pltpu.VMEM((4, 2, ROWS, GROUP), BF16),
            pltpu.VMEM((3, ROWS, WIDE), BF16),
            pltpu.VMEM((3, ROWS, WIDE), BF16),
            pltpu.VMEM((ROWS, WIDE), BF16),
            pltpu.VMEM((ROWS, GROUP), BF16),
            pltpu.SemaphoreType.DMA((COPIES,)),
            pltpu.SemaphoreType.DMA((COPIES,)),
            pltpu.SemaphoreType.DMA((LOCALS,)),
        ],
        compiler_params=pltpu.CompilerParams(
            collective_id=0, has_side_effects=True, vmem_limit_bytes=60 * 1024 * 1024
        ),
        name="layer",
    )(
        hidden,
        seg_ids.reshape(1, ROWS),
        jnp.transpose(modulation[0], (1, 0, 2)),
        qk_gain,
        jnp.transpose(w_qkv, (1, 0, 2)),
        w_mlp_in,
        w_out,
        w_mlp_back,
    )
    return guided.reshape(ROWS, 1, 1, GROUP)


def solution(mesh):
    in_specs = (
        P("seq", "tp"),
        P("seq"),
        P("guide", None, None, None),
        P(),
        P(None, None, "tp"),
        P("seq", "tp"),
        P("tp", None),
        P("seq", "tp"),
    )
    out_specs = P("seq", "tp", "guide", None)
    return jax.shard_map(
        on_device, mesh=mesh, in_specs=in_specs, out_specs=out_specs, check_vma=False
    )
```

time: 260 us -> 79.2 us (0.30)
  the two profiles are of different devices: /device:TPU:4 before, /device:TPU:1 now
where the time goes in v2:
time: 79.2 us; the launch traced here: 79.1 us
  Pallas kernels  77.6 us (98%)
  local copies, waits for them, and re-layouts  1.42 us (2%)
    pallas_call x1, Pallas kernels, on_device(): pl.pallas_call(body, out_shape=jax.ShapeDtypeStruct((ROWS, GROUP), BF16),...  77.6 us

profile of v2, /device:TPU:1, one launch (start us, length us, event | category | flops | bytes accessed | tf_op | source)
XLA Modules:
  0.0 79.1 jit_solution(14323650321837968079)
XLA Ops:
  0.0 77.6 %layer.1 = bf16[64,384]{1,0:T(8,128)(2,1)} custom-call(bf16[64,768]{1,0:T(8,128)(2,1)} %hidden.1, s32[1,64]{1,0:T(1,128)} %bitcast.9, bf16[3,4,3072]{2,1,0:T(4,128)(2,1)} %bitcast.8, f32[2,128]{1,0:T(2,128)} %qk_gain.1, bf16[3,3072,384]{2,1,0:T(8,128)(2,1)} %bitcast.6, bf16[96,1536]{1,0:T(8,128)(2,1)} %w_in.1, bf16[384,3072]{1,0:T(8,128)(2,1)} %w_out.1, ...), custom_call_target="tpu_custom_call" | custom-call | tf_op jit(solution)/shard_map/layer/pallas_call | solution.py:409
  77.6 1.4 %copy.10 = bf16[64,1,1,384]{3,0,2,1:T(8,128)(2,1)} copy(bf16[64,1,1,384]{3,0,2,1:T(8,128)(2,1)} %bitcast.7) | data formatting | bytes 98304

commit v3 on v2

v3 whole, which is shorter than its diff:
```python
import jax
import jax.numpy as jnp
from jax import lax
from jax.experimental import pallas as pl
from jax.experimental.pallas import tpu as pltpu
from jax.sharding import PartitionSpec as P

D = 3072
HEAD = 128
ROWS = 64
WIDE = 768
GROUP = 384
SLAB = 96
HEADS_HERE = 3
REQUESTS = 4
KV = 2 * GROUP + HEAD
GUIDANCE = 3.5
COPIES = 96
LOCALS = 10

F32 = jnp.float32
BF16 = jnp.bfloat16


def dot(a, b):
    return jnp.dot(a, b, preferred_element_type=F32)


def dot_t(a, b):
    return lax.dot_general(a, b, (((1,), (1,)), ((), ())), preferred_element_type=F32)


class Links:
    def __init__(self, send_sems, recv_sems):
        self.send_sems, self.recv_sems = send_sems, recv_sems
        self.used = 0
        self.sent = []

    def copy(self, src, dst, device):
        i = self.used
        self.used += 1
        made = pltpu.make_async_remote_copy(
            src_ref=src,
            dst_ref=dst,
            send_sem=self.send_sems.at[i],
            recv_sem=self.recv_sems.at[i],
            device_id=device,
            device_id_type=pl.DeviceIdType.MESH,
        )
        self.sent.append(made)
        return made

    def drain(self):
        for made in self.sent:
            made.wait_send()


class RingGather:
    def __init__(self, links, right, left, own, at_right, at_left, from_left, from_right, on_right, on_left):
        self.first = [
            links.copy(own(0), at_right(0), right),
            links.copy(own(1), at_left(1), left),
            links.copy(own(1), at_right(1), right),
            links.copy(own(0), at_left(0), left),
        ]
        self.onward = [
            links.copy(from_left(0), on_right(0), right),
            links.copy(from_right(1), on_left(1), left),
        ]

    def start(self):
        for made in self.first:
            made.start()

    def forward(self):
        self.first[0].wait_recv()
        self.onward[0].start()
        self.first[1].wait_recv()
        self.onward[1].start()

    def near(self):
        self.first[2].wait_recv()
        self.first[3].wait_recv()

    def far(self):
        self.onward[0].wait_recv()
        self.onward[1].wait_recv()

    def finish(self):
        self.near()
        self.far()


def body(
    hidden, seg, modulation, qk_gain, w_qkv, w_in, w_out, w_back,
    result,
    raw, xm, win, wback, kv, wqkv_v, wout_v, mod_v, gain_v, seg_x, qx, peak_v, part_out, part_in,
    act, mlp_out, mlp_in, z_out, z_in, own_out, other_out,
    send_sems, recv_sems, local_sems,
):
    g = lax.axis_index("guide")
    s = lax.axis_index("seq")
    t = lax.axis_index("tp")
    x, y, c = s // 8, (s % 8) // 2, s % 2
    yr, yl = (y + 1) % 4, (y + 3) % 4

    def at_seq(xx, yy, cc):
        return {"seq": xx * 8 + yy * 2 + cc}

    x_right, x_left, x_far = at_seq((x + 1) % 4, y, c), at_seq((x + 3) % 4, y, c), at_seq((x + 2) % 4, y, c)
    y_right, y_left = at_seq(x, yr, c), at_seq(x, yl, c)
    mate = at_seq(x, y, 1 - c)
    t_right, t_left, t_far = {"tp": (t + 1) % 4}, {"tp": (t + 3) % 4}, {"tp": (t + 2) % 4}
    partner = {"guide": 1 - g}

    barrier = pltpu.get_barrier_semaphore()
    everyone = (x_right, x_left, x_far, y_right, y_left, mate, t_right, t_left, t_far, partner)
    for device in everyone:
        pl.semaphore_signal(barrier, inc=1, device_id=device, device_id_type=pl.DeviceIdType.MESH)

    def columns(weight, dx, h=None):
        cols = pl.ds(pl.multiple_of(((x + dx) % 4) * GROUP, GROUP), GROUP)
        return weight.at[:, cols] if h is None else weight.at[pl.ds(h * 48, 48), cols]

    pairs = [
        (hidden, raw.at[0, 0]),
        (seg, seg_x.at[0]),
        (modulation, mod_v),
        (qk_gain, gain_v),
        (w_qkv.at[1], wqkv_v.at[1]),
        (w_qkv.at[2], wqkv_v.at[2]),
        (w_qkv.at[0], wqkv_v.at[0]),
        (columns(w_in, 0), win.at[0, y, c]),
        (w_back, wback.at[y, c]),
        (w_out, wout_v),
    ]
    local = [pltpu.make_async_copy(a, b, local_sems.at[i]) for i, (a, b) in enumerate(pairs)]
    for made in local:
        made.start()
    pl.semaphore_wait(barrier, len(everyone))

    links = Links(send_sems, recv_sems)
    half32 = lambda h: pl.ds(h * 32, 32)
    half48 = lambda h: pl.ds(h * 48, 48)
    two = lambda h: pl.ds(h * 2, 2)

    def relative(right, left, spot, own=None):
        spots = [(lambda d: (lambda h: spot(d, h)))(d) for d in (3, 1, 3, 1, 2, 2)]
        return RingGather(links, right, left, own or (lambda h: spot(0, h)), *spots)

    def absolute(spot, own=None):
        spots = [(lambda yy: (lambda h: spot(yy, h)))(yy) for yy in (y, y, yl, yr, yl, yr)]
        return RingGather(links, y_right, y_left, own or (lambda h: spot(y, h)), *spots)

    over_tp = relative(t_right, t_left, lambda d, h: raw.at[0, d, half32(h)], lambda h: hidden.at[half32(h)])
    over_x = [
        relative(
            x_right, x_left, (lambda k: (lambda d, h: raw.at[d, k, half32(h)]))(k),
            (lambda h: hidden.at[half32(h)]) if k == 0 else None,
        )
        for k in range(4)
    ]
    seg_sent = [
        links.copy(seg, seg_x.at[3], x_right),
        links.copy(seg, seg_x.at[1], x_left),
        links.copy(seg, seg_x.at[2], x_far),
    ]
    win_sent = [
        links.copy(columns(w_in, 2), win.at[2, y, c], x_far),
        links.copy(columns(w_in, 1), win.at[3, y, c], x_right),
        links.copy(columns(w_in, 3), win.at[1, y, c], x_left),
    ]
    win_near = absolute(lambda yy, h: win.at[0, yy, c, half48(h)], lambda h: columns(w_in, 0, h))
    win_rest = absolute(lambda yy, h: win.at[1:4, yy, c, half48(h)])
    wback_all = absolute(lambda yy, h: wback.at[yy, c, half48(h)], lambda h: w_back.at[half48(h)])
    win_over = [
        links.copy(win.at[0:1, :, c], win.at[0:1, :, c], mate),
        links.copy(win.at[1:4, :, c], win.at[1:4, :, c], mate),
    ]
    wback_over = links.copy(wback.at[:, c], wback.at[:, c], mate)
    kv_all = absolute(lambda yy, h: kv.at[yy, c, half32(h)])
    kv_over = links.copy(kv.at[:, c], kv.at[:, c], mate)
    q_all = relative(x_right, x_left, lambda d, h: qx.at[d, half32(h)])
    act_all = relative(x_right, x_left, lambda d, h: act.at[d, two(h)])

    over_tp.start()
    over_x[0].start()
    for made in seg_sent + win_sent:
        made.start()
    win_near.start()
    wback_all.start()

    over_tp.forward()
    over_tp.near()
    over_x[3].start()
    over_x[1].start()
    over_x[0].forward()
    win_near.forward()
    for made in win_sent:
        made.wait_recv()
    win_rest.start()
    for made in local[:4]:
        made.wait()
    for made in seg_sent:
        made.wait_recv()
    over_tp.far()
    over_x[2].start()

    at_row = lax.broadcasted_iota(jnp.int32, (ROWS, ROWS), 0)
    at_col = lax.broadcasted_iota(jnp.int32, (ROWS, ROWS), 1)
    lane = lax.broadcasted_iota(jnp.int32, (ROWS, HEAD), 1).astype(F32)

    def seg_column(d):
        row = jnp.broadcast_to(seg_x[d].astype(F32), (ROWS, ROWS))
        return jnp.sum(jnp.where(at_row == at_col, row, 0.0), axis=-1, keepdims=True)

    seg_cols = [seg_column(d) for d in range(4)]
    one_hots = [jnp.where(seg_cols[d] == lane, 1.0, 0.0).astype(BF16) for d in range(4)]

    def look_up(kind, offset, d):
        table = mod_v[kind, :, pl.ds(pl.multiple_of(offset, WIDE), WIDE)].astype(F32)
        found = jnp.broadcast_to(table[0:1], (ROWS, WIDE))
        for r in range(1, REQUESTS):
            found = jnp.where(seg_cols[d] == float(r), table[r : r + 1], found)
        return found

    def normalise(d):
        total = sum(jnp.sum(raw[d, k].astype(F32), axis=-1, keepdims=True) for k in range(4))
        mean = total * (1.0 / D)
        squares = jnp.zeros((ROWS, 1), F32)
        for k in range(4):
            centred = raw[d, k].astype(F32) - mean
            squares += jnp.sum(centred * centred, axis=-1, keepdims=True)
        scale_rows = lax.rsqrt(squares * (1.0 / D) + 1e-06)
        for k in range(4):
            offset = ((t + k) % 4) * WIDE
            normed = (raw[d, k].astype(F32) - mean) * scale_rows
            xm[d, :, pl.ds(pl.multiple_of(offset, WIDE), WIDE)] = (
                normed * (1.0 + look_up(1, offset, d)) + look_up(0, offset, d)
            ).astype(BF16)

    normalise(0)
    over_x[3].forward()
    over_x[1].forward()

    def head_norm(values, gain):
        return values * lax.rsqrt(jnp.mean(values * values, axis=-1, keepdims=True) + 1e-06) * gain

    rows_own = xm[0]
    local[4].wait()
    keys = dot(rows_own, wqkv_v[1])
    for h in range(HEADS_HERE):
        cols = slice(h * HEAD, (h + 1) * HEAD)
        kv[y, c, :, cols] = head_norm(keys[:, cols], gain_v[1:2, :]).astype(BF16)
    win_rest.forward()
    wback_all.forward()
    local[5].wait()
    kv[y, c, :, GROUP : 2 * GROUP] = dot(rows_own, wqkv_v[2]).astype(BF16)
    kv[y, c, :, 2 * GROUP :] = one_hots[0]
    kv_all.start()
    over_x[2].forward()
    local[6].wait()
    query = dot(rows_own, wqkv_v[0])
    for h in range(HEADS_HERE):
        cols = slice(h * HEAD, (h + 1) * HEAD)
        qx[0, :, cols] = head_norm(query[:, cols], gain_v[0:1, :]).astype(BF16)
    q_all.start()

    local[7].wait()
    win_near.finish()
    win_over[0].start()
    win_rest.finish()
    win_over[1].start()
    over_x[0].finish()
    over_x[1].finish()
    over_x[3].finish()
    over_x[2].finish()
    normalise(1)
    kv_all.forward()
    normalise(3)
    q_all.forward()
    normalise(2)
    for made in win_over:
        made.wait_recv()

    pre = jnp.zeros((4 * ROWS, GROUP), F32)
    for d in range(4):
        cols = pl.ds(pl.multiple_of(((x + d) % 4) * WIDE, WIDE), WIDE)
        pre += dot(xm[:, :, cols].reshape(4 * ROWS, WIDE), win[d].reshape(WIDE, GROUP))
    acted = jax.nn.gelu(pre, approximate=True).astype(BF16)
    for d in range(4):
        act[0, (x + d) % 4] = acted[d * ROWS : (d + 1) * ROWS]
    act_all.start()

    local[8].wait()
    wback_all.finish()
    wback_over.start()
    kv_all.finish()
    kv_over.start()
    q_all.finish()
    kv_over.wait_recv()

    seen = kv.reshape(8 * ROWS, KV)
    same = dot_t(jnp.concatenate(one_hots, axis=0), seen[:, 2 * GROUP :]) > 0.5
    lanes = lax.broadcasted_iota(jnp.int32, (4 * ROWS, HEAD), 1)
    stats = jnp.zeros((4 * ROWS, HEAD), F32)
    for h in range(HEADS_HERE):
        k_cols = slice(h * HEAD, (h + 1) * HEAD)
        v_cols = slice(GROUP + h * HEAD, GROUP + (h + 1) * HEAD)
        score = dot_t(qx[:, :, k_cols].reshape(4 * ROWS, HEAD), seen[:, k_cols]) * HEAD ** (-0.5)
        score = jnp.where(same, score, -1e30)
        peak_v[...] = jnp.broadcast_to(jnp.max(score, axis=-1, keepdims=True), (4 * ROWS, HEAD)).astype(BF16)
        peak = peak_v[:, 0:1].astype(F32)
        weight = jnp.where(same, jnp.exp(score - peak), 0.0)
        total = jnp.sum(weight, axis=-1, keepdims=True)
        summed = dot(weight.astype(BF16), seen[:, v_cols])
        part = (summed / jnp.where(total > 0.0, total, 1.0)).astype(BF16)
        part_out[:, :, k_cols] = part.reshape(4, ROWS, HEAD)
        upper = total.astype(BF16).astype(F32)
        stats = jnp.where(lanes == h, peak, stats)
        stats = jnp.where(lanes == 3 + h, upper, stats)
        stats = jnp.where(lanes == 6 + h, total - upper, stats)
        if h == 0:
            act_all.forward()
    part_out[:, :, GROUP:] = stats.astype(BF16).reshape(4, ROWS, HEAD)
    part_sent = [
        links.copy(part_out.at[2], part_in.at[2], x_far),
        links.copy(part_out.at[1], part_in.at[3], x_right),
        links.copy(part_out.at[3], part_in.at[1], x_left),
    ]
    for made in part_sent:
        made.start()
    wback_over.wait_recv()

    def back(d):
        cols = pl.ds(pl.multiple_of(((x + d) % 4) * GROUP, GROUP), GROUP)
        return dot_t(act[d].reshape(4 * ROWS, GROUP), wback[:, :, :, cols].reshape(WIDE, GROUP))

    fed = back(0)
    act_all.near()
    fed += back(1)
    fed += back(3)
    act_all.far()
    fed += back(2)
    for b in range(4):
        mlp_out[(b - x + 4) % 4] = fed[b * ROWS : (b + 1) * ROWS].astype(BF16)
    mlp_sent = {
        2: links.copy(mlp_out.at[2], mlp_in.at[2], x_far),
        3: links.copy(mlp_out.at[1], mlp_in.at[3], x_right),
        1: links.copy(mlp_out.at[3], mlp_in.at[1], x_left),
    }
    for made in mlp_sent.values():
        made.start()

    for made in part_sent:
        made.wait_recv()
    attended = []
    for h in range(HEADS_HERE):
        cols = slice(h * HEAD, (h + 1) * HEAD)
        parts = [part_out[0]] + [part_in[d] for d in (1, 2, 3)]
        stat = [p[:, GROUP:].astype(F32) for p in parts]
        top = stat[0][:, h : h + 1]
        for other in stat[1:]:
            top = jnp.maximum(top, other[:, h : h + 1])
        total = jnp.zeros((ROWS, 1), F32)
        summed = jnp.zeros((ROWS, HEAD), F32)
        for p, st in zip(parts, stat):
            share = jnp.exp(st[:, h : h + 1] - top) * (st[:, 3 + h : 4 + h] + st[:, 6 + h : 7 + h])
            total += share
            summed += share * p[:, cols].astype(F32)
        attended.append((summed / total).astype(BF16))
    attended = jnp.concatenate(attended, axis=1)
    local[9].wait()

    steps = [
        links.copy(z_out.at[0], z_in.at[step - 1], {"tp": (t + step) % 4}) for step in (1, 2, 3)
    ]
    first_sem = links.used - 3
    for d in (0, 1, 3, 2):
        e = (x + d) % 4
        term = dot(attended, wout_v[:, pl.ds(pl.multiple_of(e * WIDE, WIDE), WIDE)])
        if d == 0:
            term += mlp_out[0].astype(F32)
        else:
            mlp_sent[d].wait_recv()
            term += mlp_in[d].astype(F32)
        z_out[d] = term.astype(BF16)
        for step in (1, 2, 3):

            @pl.when((e - t + 4) % 4 == step)
            def _():
                pltpu.make_async_remote_copy(
                    src_ref=z_out.at[d],
                    dst_ref=z_in.at[step - 1],
                    send_sem=send_sems.at[first_sem + step - 1],
                    recv_sem=recv_sems.at[first_sem + step - 1],
                    device_id={"tp": (t + step) % 4},
                    device_id_type=pl.DeviceIdType.MESH,
                ).start()

    gate = look_up(2, t * WIDE, 0)
    branch = z_out[(t - x + 4) % 4].astype(F32)
    for k, made in enumerate(steps):
        made.wait_recv()
        branch += z_in[k].astype(F32)
    own_out[...] = (raw[0, 0].astype(F32) + gate * branch).astype(BF16)
    kept_cols = pl.ds(pl.multiple_of(g * GROUP, GROUP), GROUP)
    handed_cols = pl.ds(pl.multiple_of((1 - g) * GROUP, GROUP), GROUP)
    swap = links.copy(own_out.at[:, handed_cols], other_out, partner)
    swap.start()
    kept = own_out[:, kept_cols].astype(F32)
    swap.wait_recv()
    other = other_out[...].astype(F32)
    cond = jnp.where(g == 0, kept, other)
    uncond = jnp.where(g == 0, other, kept)
    result[...] = (uncond + GUIDANCE * (cond - uncond)).astype(BF16)
    links.drain()


def on_device(hidden, seg_ids, modulation, qk_gain, w_qkv, w_mlp_in, w_out, w_mlp_back):
    anywhere = pl.BlockSpec(memory_space=pl.ANY)
    guided = pl.pallas_call(
        body,
        out_shape=jax.ShapeDtypeStruct((ROWS, GROUP), BF16),
        in_specs=[anywhere] * 8,
        out_specs=pl.BlockSpec(memory_space=pltpu.VMEM),
        scratch_shapes=[
            pltpu.VMEM((4, 4, ROWS, WIDE), BF16),
            pltpu.VMEM((4, ROWS, D), BF16),
            pltpu.VMEM((4, 4, 2, SLAB, GROUP), BF16),
            pltpu.VMEM((4, 2, SLAB, 4 * GROUP), BF16),
            pltpu.VMEM((4, 2, ROWS, KV), BF16),
            pltpu.VMEM((3, D, GROUP), BF16),
            pltpu.VMEM((GROUP, D), BF16),
            pltpu.VMEM((3, REQUESTS, D), BF16),
            pltpu.VMEM((2, HEAD), F32),
            pltpu.VMEM((4, 1, ROWS), jnp.int32),
            pltpu.VMEM((4, ROWS, GROUP), BF16),
            pltpu.VMEM((4 * ROWS, HEAD), BF16),
            pltpu.VMEM((4, ROWS, GROUP + HEAD), BF16),
            pltpu.VMEM((4, ROWS, GROUP + HEAD), BF16),
            pltpu.VMEM((4, 4, ROWS, GROUP), BF16),
            pltpu.VMEM((4, ROWS, WIDE), BF16),
            pltpu.VMEM((4, ROWS, WIDE), BF16),
            pltpu.VMEM((4, ROWS, WIDE), BF16),
            pltpu.VMEM((3, ROWS, WIDE), BF16),
            pltpu.VMEM((ROWS, WIDE), BF16),
            pltpu.VMEM((ROWS, GROUP), BF16),
            pltpu.SemaphoreType.DMA((COPIES,)),
            pltpu.SemaphoreType.DMA((COPIES,)),
            pltpu.SemaphoreType.DMA((LOCALS,)),
        ],
        compiler_params=pltpu.CompilerParams(
            collective_id=0, has_side_effects=True, vmem_limit_bytes=60 * 1024 * 1024
        ),
        name="layer",
    )(
        hidden,
        seg_ids.reshape(1, ROWS),
        jnp.transpose(modulation[0], (1, 0, 2)),
        qk_gain,
        jnp.transpose(w_qkv, (1, 0, 2)),
        w_mlp_in,
        w_out,
        w_mlp_back,
    )
    return guided.reshape(ROWS, 1, 1, GROUP)


def solution(mesh):
    in_specs = (
        P("seq", "tp"),
        P("seq"),
        P("guide", None, None, None),
        P(),
        P(None, None, "tp"),
        P("seq", "tp"),
        P("tp", None),
        P("seq", "tp"),
    )
    out_specs = P("seq", "tp", "guide", None)
    return jax.shard_map(
        on_device, mesh=mesh, in_specs=in_specs, out_specs=out_specs, check_vma=False
    )
```

time: 79.2 us -> 68.2 us (0.86)
  the two profiles are of different devices: /device:TPU:1 before, /device:TPU:4 now
where the time goes in v3:
time: 68.2 us; the launch traced here: 67.2 us
  Pallas kernels  65.8 us (96%)
  local copies, waits for them, and re-layouts  1.42 us (2%)
    pallas_call x1, Pallas kernels, on_device(): pl.pallas_call(body, out_shape=jax.ShapeDtypeStruct((ROWS, GROUP), BF16),...  65.8 us
    unnamed x1, local copies, waits for them, and re-layouts  1.42 us

profile of v3, /device:TPU:4, one launch (start us, length us, event | category | flops | bytes accessed | tf_op | source)
XLA Modules:
  0.0 67.2 jit_solution(18222255041260333603)
XLA Ops:
  0.0 65.8 %layer.1 = bf16[64,384]{1,0:T(8,128)(2,1)} custom-call(bf16[64,768]{1,0:T(8,128)(2,1)} %hidden.1, s32[1,64]{1,0:T(1,128)} %bitcast.9, bf16[3,4,3072]{2,1,0:T(4,128)(2,1)} %bitcast.8, f32[2,128]{1,0:T(2,128)} %qk_gain.1, bf16[3,3072,384]{2,1,0:T(8,128)(2,1)} %bitcast.6, bf16[96,1536]{1,0:T(8,128)(2,1)} %w_in.1, bf16[384,3072]{1,0:T(8,128)(2,1)} %w_out.1, ...), custom_call_target="tpu_custom_call" | custom-call | tf_op jit(solution)/shard_map/layer/pallas_call | solution.py:422
  65.8 1.4 %copy.10 = bf16[64,1,1,384]{3,0,2,1:T(8,128)(2,1)} copy(bf16[64,1,1,384]{3,0,2,1:T(8,128)(2,1)} %bitcast.7) | data formatting | bytes 98304

commit v4 on v3

--- a/solution.py
+++ b/solution.py
@@ -68,9 +68,17 @@
             links.copy(from_right(1), on_left(1), left),
         ]
 
+    def begin(self):
+        self.first[0].start()
+        self.first[1].start()
+
+    def follow(self):
+        self.first[2].start()
+        self.first[3].start()
+
     def start(self):
-        for made in self.first:
-            made.start()
+        self.begin()
+        self.follow()
 
     def forward(self):
         self.first[0].wait_recv()
@@ -95,7 +103,7 @@
     hidden, seg, modulation, qk_gain, w_qkv, w_in, w_out, w_back,
     result,
     raw, xm, win, wback, kv, wqkv_v, wout_v, mod_v, gain_v, seg_x, qx, peak_v, part_out, part_in,
-    act, mlp_out, mlp_in, z_out, z_in, own_out, other_out,
+    act, mlp_out, mlp_in, z_out, z_in, gate_in,
     send_sems, recv_sems, local_sems,
 ):
     g = lax.axis_index("guide")
@@ -112,9 +120,10 @@
     mate = at_seq(x, y, 1 - c)
     t_right, t_left, t_far = {"tp": (t + 1) % 4}, {"tp": (t + 3) % 4}, {"tp": (t + 2) % 4}
     partner = {"guide": 1 - g}
+    across = [{"guide": 1 - g, "tp": (t + step) % 4} for step in (1, 2, 3)]
 
     barrier = pltpu.get_barrier_semaphore()
-    everyone = (x_right, x_left, x_far, y_right, y_left, mate, t_right, t_left, t_far, partner)
+    everyone = (x_right, x_left, x_far, y_right, y_left, mate, t_right, t_left, t_far, partner, *across)
     for device in everyone:
         pl.semaphore_signal(barrier, inc=1, device_id=device, device_id_type=pl.DeviceIdType.MESH)
 
@@ -183,19 +192,24 @@
     q_all = relative(x_right, x_left, lambda d, h: qx.at[d, half32(h)])
     act_all = relative(x_right, x_left, lambda d, h: act.at[d, two(h)])
 
+    gate_sent = links.copy(
+        modulation.at[2, :, pl.ds(pl.multiple_of(t * WIDE + (1 - g) * GROUP, GROUP), GROUP)], gate_in, partner
+    )
+
     over_tp.start()
     over_x[0].start()
     for made in seg_sent + win_sent:
         made.start()
     win_near.start()
-    wback_all.start()
-
+    wback_all.begin()
+    gate_sent.start()
+
+    win_near.forward()
     over_tp.forward()
+    over_x[0].forward()
     over_tp.near()
     over_x[3].start()
     over_x[1].start()
-    over_x[0].forward()
-    win_near.forward()
     for made in win_sent:
         made.wait_recv()
     win_rest.start()
@@ -253,12 +267,12 @@
         cols = slice(h * HEAD, (h + 1) * HEAD)
         kv[y, c, :, cols] = head_norm(keys[:, cols], gain_v[1:2, :]).astype(BF16)
     win_rest.forward()
-    wback_all.forward()
     local[5].wait()
     kv[y, c, :, GROUP : 2 * GROUP] = dot(rows_own, wqkv_v[2]).astype(BF16)
     kv[y, c, :, 2 * GROUP :] = one_hots[0]
     kv_all.start()
     over_x[2].forward()
+    wback_all.follow()
     local[6].wait()
     query = dot(rows_own, wqkv_v[0])
     for h in range(HEADS_HERE):
@@ -271,14 +285,15 @@
     win_over[0].start()
     win_rest.finish()
     win_over[1].start()
-    over_x[0].finish()
-    over_x[1].finish()
-    over_x[3].finish()
-    over_x[2].finish()
+    kv_all.forward()
+    wback_all.forward()
+    for k in (0, 1, 3, 2):
+        over_x[k].finish()
     normalise(1)
-    kv_all.forward()
+    q_all.forward()
     normalise(3)
-    q_all.forward()
+    kv_all.finish()
+    kv_over.start()
     normalise(2)
     for made in win_over:
         made.wait_recv()
@@ -292,11 +307,6 @@
         act[0, (x + d) % 4] = acted[d * ROWS : (d + 1) * ROWS]
     act_all.start()
 
-    local[8].wait()
-    wback_all.finish()
-    wback_over.start()
-    kv_all.finish()
-    kv_over.start()
     q_all.finish()
     kv_over.wait_recv()
 
@@ -321,6 +331,10 @@
         stats = jnp.where(lanes == 3 + h, upper, stats)
         stats = jnp.where(lanes == 6 + h, total - upper, stats)
         if h == 0:
+            local[8].wait()
+            wback_all.finish()
+            wback_over.start()
+        if h == 1:
             act_all.forward()
     part_out[:, :, GROUP:] = stats.astype(BF16).reshape(4, ROWS, HEAD)
     part_sent = [
@@ -372,12 +386,23 @@
     attended = jnp.concatenate(attended, axis=1)
     local[9].wait()
 
-    steps = [
-        links.copy(z_out.at[0], z_in.at[step - 1], {"tp": (t + step) % 4}) for step in (1, 2, 3)
-    ]
-    first_sem = links.used - 3
+    base = links.used
+    own_cols = pl.ds(pl.multiple_of(g * GROUP, GROUP), GROUP)
+    other_cols = pl.ds(pl.multiple_of((1 - g) * GROUP, GROUP), GROUP)
+
+    def term_copy(d, kind, step):
+        return pltpu.make_async_remote_copy(
+            src_ref=z_out.at[d, :, (own_cols, other_cols)[kind]],
+            dst_ref=z_in.at[kind, step],
+            send_sem=send_sems.at[base + 4 * kind + step],
+            recv_sem=recv_sems.at[base + 4 * kind + step],
+            device_id={"guide": (g, 1 - g)[kind], "tp": (t + step) % 4},
+            device_id_type=pl.DeviceIdType.MESH,
+        )
+
     for d in (0, 1, 3, 2):
         e = (x + d) % 4
+        step = (x + d - t + 4) % 4
         term = dot(attended, wout_v[:, pl.ds(pl.multiple_of(e * WIDE, WIDE), WIDE)])
         if d == 0:
             term += mlp_out[0].astype(F32)
@@ -385,35 +410,40 @@
             mlp_sent[d].wait_recv()
             term += mlp_in[d].astype(F32)
         z_out[d] = term.astype(BF16)
-        for step in (1, 2, 3):
-
-            @pl.when((e - t + 4) % 4 == step)
-            def _():
-                pltpu.make_async_remote_copy(
-                    src_ref=z_out.at[d],
-                    dst_ref=z_in.at[step - 1],
-                    send_sem=send_sems.at[first_sem + step - 1],
-                    recv_sem=recv_sems.at[first_sem + step - 1],
-                    device_id={"tp": (t + step) % 4},
-                    device_id_type=pl.DeviceIdType.MESH,
-                ).start()
-
-    gate = look_up(2, t * WIDE, 0)
-    branch = z_out[(t - x + 4) % 4].astype(F32)
-    for k, made in enumerate(steps):
+        term_copy(d, 1, step).start()
+
+        @pl.when(step != 0)
+        def _():
+            term_copy(d, 0, step).start()
+
+    gate_sent.wait_recv()
+    own_table = mod_v[2, :, pl.ds(pl.multiple_of(t * WIDE + g * GROUP, GROUP), GROUP)].astype(F32)
+    other_table = gate_in[...].astype(F32)
+
+    def gate_of(table):
+        found = jnp.broadcast_to(table[0:1], (ROWS, GROUP))
+        for r in range(1, REQUESTS):
+            found = jnp.where(seg_cols[0] == float(r), table[r : r + 1], found)
+        return found
+
+    own_gate, other_gate = gate_of(own_table), gate_of(other_table)
+    residual = raw[0, 0, :, own_cols].astype(F32)
+    own_branch = z_out[(t - x + 4) % 4, :, own_cols].astype(F32)
+    arrived = [term_copy(0, 0, step) for step in (1, 2, 3)] + [term_copy(0, 1, step) for step in range(4)]
+    for made in arrived:
         made.wait_recv()
-        branch += z_in[k].astype(F32)
-    own_out[...] = (raw[0, 0].astype(F32) + gate * branch).astype(BF16)
-    kept_cols = pl.ds(pl.multiple_of(g * GROUP, GROUP), GROUP)
-    handed_cols = pl.ds(pl.multiple_of((1 - g) * GROUP, GROUP), GROUP)
-    swap = links.copy(own_out.at[:, handed_cols], other_out, partner)
-    swap.start()
-    kept = own_out[:, kept_cols].astype(F32)
-    swap.wait_recv()
-    other = other_out[...].astype(F32)
-    cond = jnp.where(g == 0, kept, other)
-    uncond = jnp.where(g == 0, other, kept)
+    for step in (1, 2, 3):
+        own_branch += z_in[0, step].astype(F32)
+    other_branch = z_in[1, 0].astype(F32)
+    for step in (1, 2, 3):
+        other_branch += z_in[1, step].astype(F32)
+    mine = (residual + own_gate * own_branch).astype(BF16).astype(F32)
+    theirs = (residual + other_gate * other_branch).astype(BF16).astype(F32)
+    cond = jnp.where(g == 0, mine, theirs)
+    uncond = jnp.where(g == 0, theirs, mine)
     result[...] = (uncond + GUIDANCE * (cond - uncond)).astype(BF16)
+    for made in arrived:
+        made.wait_send()
     links.drain()
 
 
@@ -443,9 +473,8 @@
             pltpu.VMEM((4, ROWS, WIDE), BF16),
             pltpu.VMEM((4, ROWS, WIDE), BF16),
             pltpu.VMEM((4, ROWS, WIDE), BF16),
-            pltpu.VMEM((3, ROWS, WIDE), BF16),
-            pltpu.VMEM((ROWS, WIDE), BF16),
-            pltpu.VMEM((ROWS, GROUP), BF16),
+            pltpu.VMEM((2, 4, ROWS, GROUP), BF16),
+            pltpu.VMEM((REQUESTS, GROUP), BF16),
             pltpu.SemaphoreType.DMA((COPIES,)),
             pltpu.SemaphoreType.DMA((COPIES,)),
             pltpu.SemaphoreType.DMA((LOCALS,)),

time: 68.2 us -> 63.4 us (0.930); the launches traced: 67.2 us -> 63.3 us
  Pallas kernels: 65.8 us -> 61.9 us
    pallas_call x1, Pallas kernels: 65.8 us -> 61.9 us  [on_device(): pl.pallas_call(body, out_shape=jax.ShapeDtypeStruct((ROWS, GROUP), BF16),...]
where the time goes in v4:
time: 63.4 us; the launch traced here: 63.3 us
  Pallas kernels  61.9 us (98%)
  local copies, waits for them, and re-layouts  1.42 us (2%)
    pallas_call x1, Pallas kernels, on_device(): pl.pallas_call(body, out_shape=jax.ShapeDtypeStruct((ROWS, GROUP), BF16),...  61.9 us
    unnamed x1, local copies, waits for them, and re-layouts  1.42 us

profile of v4, /device:TPU:4, one launch (start us, length us, event | category | flops | bytes accessed | tf_op | source)
XLA Modules:
  0.0 63.3 jit_solution(1076756429475975065)
XLA Ops:
  0.0 61.9 %layer.1 = bf16[64,384]{1,0:T(8,128)(2,1)} custom-call(bf16[64,768]{1,0:T(8,128)(2,1)} %hidden.1, s32[1,64]{1,0:T(1,128)} %bitcast.9, bf16[3,4,3072]{2,1,0:T(4,128)(2,1)} %bitcast.8, f32[2,128]{1,0:T(2,128)} %qk_gain.1, bf16[3,3072,384]{2,1,0:T(8,128)(2,1)} %bitcast.6, bf16[96,1536]{1,0:T(8,128)(2,1)} %w_in.1, bf16[384,3072]{1,0:T(8,128)(2,1)} %w_out.1, ...), custom_call_target="tpu_custom_call" | custom-call | tf_op jit(solution)/shard_map/layer/pallas_call | solution.py:452
  61.9 1.4 %copy.10 = bf16[64,1,1,384]{3,0,2,1:T(8,128)(2,1)} copy(bf16[64,1,1,384]{3,0,2,1:T(8,128)(2,1)} %bitcast.7) | data formatting | bytes 98304

commit v5 on v4

--- a/solution.py
+++ b/solution.py
@@ -15,7 +15,7 @@
 REQUESTS = 4
 KV = 2 * GROUP + HEAD
 GUIDANCE = 3.5
-COPIES = 96
+COPIES = 128
 LOCALS = 10
 
 F32 = jnp.float32
@@ -175,18 +175,22 @@
         links.copy(seg, seg_x.at[2], x_far),
     ]
     win_sent = [
-        links.copy(columns(w_in, 2), win.at[2, y, c], x_far),
-        links.copy(columns(w_in, 1), win.at[3, y, c], x_right),
+        links.copy(columns(w_in, 1), win.at[2, y, c], x_right),
         links.copy(columns(w_in, 3), win.at[1, y, c], x_left),
+        links.copy(columns(w_in, 2), win.at[3, y, c], x_far),
     ]
     win_near = absolute(lambda yy, h: win.at[0, yy, c, half48(h)], lambda h: columns(w_in, 0, h))
-    win_rest = absolute(lambda yy, h: win.at[1:4, yy, c, half48(h)])
+    win_sides = absolute(lambda yy, h: win.at[1:3, yy, c, half48(h)])
+    win_rest = absolute(lambda yy, h: win.at[3, yy, c, half48(h)])
     wback_all = absolute(lambda yy, h: wback.at[yy, c, half48(h)], lambda h: w_back.at[half48(h)])
-    win_over = [
-        links.copy(win.at[0:1, :, c], win.at[0:1, :, c], mate),
-        links.copy(win.at[1:4, :, c], win.at[1:4, :, c], mate),
-    ]
-    wback_over = links.copy(wback.at[:, c], wback.at[:, c], mate)
+
+    def to_mate(spot):
+        return links.copy(spot, spot, mate)
+
+    over_first = to_mate(win.at[0, :, c])
+    over_sides = [to_mate(win.at[1:3, yy, c]) for yy in (y, yr, yl, (y + 2) % 4)]
+    over_rest = [to_mate(win.at[3, yy, c]) for yy in (y, yr, yl, (y + 2) % 4)]
+    over_back = [to_mate(wback.at[yy, c]) for yy in (y, yr, yl, (y + 2) % 4)]
     kv_all = absolute(lambda yy, h: kv.at[yy, c, half32(h)])
     kv_over = links.copy(kv.at[:, c], kv.at[:, c], mate)
     q_all = relative(x_right, x_left, lambda d, h: qx.at[d, half32(h)])
@@ -197,26 +201,37 @@
     )
 
     over_tp.start()
-    over_x[0].start()
-    for made in seg_sent + win_sent:
+    for made in win_sent:
         made.start()
     win_near.start()
-    wback_all.begin()
+    over_x[0].start()
+    for made in seg_sent:
+        made.start()
     gate_sent.start()
 
     win_near.forward()
+    win_sent[0].wait_recv()
+    win_sent[1].wait_recv()
+    win_sides.start()
+    over_sides[0].start()
     over_tp.forward()
     over_x[0].forward()
+    win_sent[2].wait_recv()
+    win_rest.start()
+    over_rest[0].start()
     over_tp.near()
     over_x[3].start()
     over_x[1].start()
-    for made in win_sent:
-        made.wait_recv()
-    win_rest.start()
+    win_sides.forward()
     for made in local[:4]:
         made.wait()
     for made in seg_sent:
         made.wait_recv()
+    win_rest.forward()
+    wback_all.begin()
+    local[7].wait()
+    win_near.finish()
+    over_first.start()
     over_tp.far()
     over_x[2].start()
 
@@ -266,13 +281,21 @@
     for h in range(HEADS_HERE):
         cols = slice(h * HEAD, (h + 1) * HEAD)
         kv[y, c, :, cols] = head_norm(keys[:, cols], gain_v[1:2, :]).astype(BF16)
-    win_rest.forward()
+    win_sides.near()
+    over_sides[1].start()
+    over_sides[2].start()
     local[5].wait()
     kv[y, c, :, GROUP : 2 * GROUP] = dot(rows_own, wqkv_v[2]).astype(BF16)
     kv[y, c, :, 2 * GROUP :] = one_hots[0]
     kv_all.start()
     over_x[2].forward()
-    wback_all.follow()
+    win_rest.near()
+    over_rest[1].start()
+    over_rest[2].start()
+    win_sides.far()
+    over_sides[3].start()
+    win_rest.far()
+    over_rest[3].start()
     local[6].wait()
     query = dot(rows_own, wqkv_v[0])
     for h in range(HEADS_HERE):
@@ -280,12 +303,10 @@
         qx[0, :, cols] = head_norm(query[:, cols], gain_v[0:1, :]).astype(BF16)
     q_all.start()
 
-    local[7].wait()
-    win_near.finish()
-    win_over[0].start()
-    win_rest.finish()
-    win_over[1].start()
     kv_all.forward()
+    wback_all.follow()
+    local[8].wait()
+    over_back[0].start()
     wback_all.forward()
     for k in (0, 1, 3, 2):
         over_x[k].finish()
@@ -295,13 +316,13 @@
     kv_all.finish()
     kv_over.start()
     normalise(2)
-    for made in win_over:
+    for made in [over_first, *over_sides, *over_rest]:
         made.wait_recv()
 
     pre = jnp.zeros((4 * ROWS, GROUP), F32)
-    for d in range(4):
+    for slot, d in enumerate((0, 1, 3, 2)):
         cols = pl.ds(pl.multiple_of(((x + d) % 4) * WIDE, WIDE), WIDE)
-        pre += dot(xm[:, :, cols].reshape(4 * ROWS, WIDE), win[d].reshape(WIDE, GROUP))
+        pre += dot(xm[:, :, cols].reshape(4 * ROWS, WIDE), win[slot].reshape(WIDE, GROUP))
     acted = jax.nn.gelu(pre, approximate=True).astype(BF16)
     for d in range(4):
         act[0, (x + d) % 4] = acted[d * ROWS : (d + 1) * ROWS]
@@ -331,9 +352,9 @@
         stats = jnp.where(lanes == 3 + h, upper, stats)
         stats = jnp.where(lanes == 6 + h, total - upper, stats)
         if h == 0:
-            local[8].wait()
-            wback_all.finish()
-            wback_over.start()
+            wback_all.near()
+            over_back[1].start()
+            over_back[2].start()
         if h == 1:
             act_all.forward()
     part_out[:, :, GROUP:] = stats.astype(BF16).reshape(4, ROWS, HEAD)
@@ -344,7 +365,10 @@
     ]
     for made in part_sent:
         made.start()
-    wback_over.wait_recv()
+    wback_all.far()
+    over_back[3].start()
+    for made in over_back:
+        made.wait_recv()
 
     def back(d):
         cols = pl.ds(pl.multiple_of(((x + d) % 4) * GROUP, GROUP), GROUP)
@@ -359,9 +383,9 @@
     for b in range(4):
         mlp_out[(b - x + 4) % 4] = fed[b * ROWS : (b + 1) * ROWS].astype(BF16)
     mlp_sent = {
-        2: links.copy(mlp_out.at[2], mlp_in.at[2], x_far),
         3: links.copy(mlp_out.at[1], mlp_in.at[3], x_right),
         1: links.copy(mlp_out.at[3], mlp_in.at[1], x_left),
+        2: links.copy(mlp_out.at[2], mlp_in.at[2], x_far),
     }
     for made in mlp_sent.values():
         made.start()

time: 63.4 us -> 61.2 us (0.965)
  Pallas kernels: 61.9 us -> 59.6 us
    pallas_call x1, Pallas kernels: 61.9 us -> 59.6 us  [on_device(): pl.pallas_call(body, out_shape=jax.ShapeDtypeStruct((ROWS, GROUP), BF16),...]
where the time goes in v5:
time: 61.2 us; the launch traced here: 61 us
  Pallas kernels  59.6 us (97%)
  local copies, waits for them, and re-layouts  1.42 us (2%)
    pallas_call x1, Pallas kernels, on_device(): pl.pallas_call(body, out_shape=jax.ShapeDtypeStruct((ROWS, GROUP), BF16),...  59.6 us
    unnamed x1, local copies, waits for them, and re-layouts  1.42 us

profile of v5, /device:TPU:4, one launch (start us, length us, event | category | flops | bytes accessed | tf_op | source)
XLA Modules:
  0.0 61.0 jit_solution(5631412026067821764)
XLA Ops:
  0.0 59.6 %layer.1 = bf16[64,384]{1,0:T(8,128)(2,1)} custom-call(bf16[64,768]{1,0:T(8,128)(2,1)} %hidden.1, s32[1,64]{1,0:T(1,128)} %bitcast.9, bf16[3,4,3072]{2,1,0:T(4,128)(2,1)} %bitcast.8, f32[2,128]{1,0:T(2,128)} %qk_gain.1, bf16[3,3072,384]{2,1,0:T(8,128)(2,1)} %bitcast.6, bf16[96,1536]{1,0:T(8,128)(2,1)} %w_in.1, bf16[384,3072]{1,0:T(8,128)(2,1)} %w_out.1, ...), custom_call_target="tpu_custom_call" | custom-call | tf_op jit(solution)/shard_map/layer/pallas_call | solution.py:476
  59.6 1.4 %copy.10 = bf16[64,1,1,384]{3,0,2,1:T(8,128)(2,1)} copy(bf16[64,1,1,384]{3,0,2,1:T(8,128)(2,1)} %bitcast.7) | data formatting | bytes 98304

commit v6 on v5

--- a/solution.py
+++ b/solution.py
@@ -8,6 +8,7 @@
 D = 3072
 HEAD = 128
 ROWS = 64
+PART = 32
 WIDE = 768
 GROUP = 384
 SLAB = 96
@@ -15,7 +16,7 @@
 REQUESTS = 4
 KV = 2 * GROUP + HEAD
 GUIDANCE = 3.5
-COPIES = 128
+COPIES = 160
 LOCALS = 10
 
 F32 = jnp.float32
@@ -103,7 +104,7 @@
     hidden, seg, modulation, qk_gain, w_qkv, w_in, w_out, w_back,
     result,
     raw, xm, win, wback, kv, wqkv_v, wout_v, mod_v, gain_v, seg_x, qx, peak_v, part_out, part_in,
-    act, mlp_out, mlp_in, z_out, z_in, gate_in,
+    act, mlp_out, mlp_in, heads_term, z_out, z_in, gate_in,
     send_sems, recv_sems, local_sems,
 ):
     g = lax.axis_index("guide")
@@ -194,7 +195,9 @@
     kv_all = absolute(lambda yy, h: kv.at[yy, c, half32(h)])
     kv_over = links.copy(kv.at[:, c], kv.at[:, c], mate)
     q_all = relative(x_right, x_left, lambda d, h: qx.at[d, half32(h)])
-    act_all = relative(x_right, x_left, lambda d, h: act.at[d, two(h)])
+    act_all = [
+        relative(x_right, x_left, (lambda r: (lambda d, h: act.at[d, r, two(h)]))(r)) for r in range(2)
+    ]
 
     gate_sent = links.copy(
         modulation.at[2, :, pl.ds(pl.multiple_of(t * WIDE + (1 - g) * GROUP, GROUP), GROUP)], gate_in, partner
@@ -325,8 +328,10 @@
         pre += dot(xm[:, :, cols].reshape(4 * ROWS, WIDE), win[slot].reshape(WIDE, GROUP))
     acted = jax.nn.gelu(pre, approximate=True).astype(BF16)
     for d in range(4):
-        act[0, (x + d) % 4] = acted[d * ROWS : (d + 1) * ROWS]
-    act_all.start()
+        for r in range(2):
+            act[0, r, (x + d) % 4] = acted[d * ROWS + r * PART : d * ROWS + (r + 1) * PART]
+    act_all[0].start()
+    act_all[1].start()
 
     q_all.finish()
     kv_over.wait_recv()
@@ -356,7 +361,7 @@
             over_back[1].start()
             over_back[2].start()
         if h == 1:
-            act_all.forward()
+            act_all[0].forward()
     part_out[:, :, GROUP:] = stats.astype(BF16).reshape(4, ROWS, HEAD)
     part_sent = [
         links.copy(part_out.at[2], part_in.at[2], x_far),
@@ -365,30 +370,35 @@
     ]
     for made in part_sent:
         made.start()
+    act_all[1].forward()
     wback_all.far()
     over_back[3].start()
     for made in over_back:
         made.wait_recv()
 
-    def back(d):
+    def back(d, r):
         cols = pl.ds(pl.multiple_of(((x + d) % 4) * GROUP, GROUP), GROUP)
-        return dot_t(act[d].reshape(4 * ROWS, GROUP), wback[:, :, :, cols].reshape(WIDE, GROUP))
-
-    fed = back(0)
-    act_all.near()
-    fed += back(1)
-    fed += back(3)
-    act_all.far()
-    fed += back(2)
-    for b in range(4):
-        mlp_out[(b - x + 4) % 4] = fed[b * ROWS : (b + 1) * ROWS].astype(BF16)
-    mlp_sent = {
-        3: links.copy(mlp_out.at[1], mlp_in.at[3], x_right),
-        1: links.copy(mlp_out.at[3], mlp_in.at[1], x_left),
-        2: links.copy(mlp_out.at[2], mlp_in.at[2], x_far),
-    }
-    for made in mlp_sent.values():
-        made.start()
+        return dot_t(act[d, r].reshape(4 * PART, GROUP), wback[:, :, :, cols].reshape(WIDE, GROUP))
+
+    def output_product(r):
+        fed = back(0, r)
+        act_all[r].near()
+        fed += back(1, r)
+        fed += back(3, r)
+        act_all[r].far()
+        fed += back(2, r)
+        for b in range(4):
+            mlp_out[r, (b - x + 4) % 4] = fed[b * PART : (b + 1) * PART].astype(BF16)
+        sent = {
+            3: links.copy(mlp_out.at[r, 1], mlp_in.at[r, 3], x_right),
+            1: links.copy(mlp_out.at[r, 3], mlp_in.at[r, 1], x_left),
+            2: links.copy(mlp_out.at[r, 2], mlp_in.at[r, 2], x_far),
+        }
+        for made in sent.values():
+            made.start()
+        return sent
+
+    mlp_sent = [output_product(0)]
 
     for made in part_sent:
         made.wait_recv()
@@ -410,35 +420,45 @@
     attended = jnp.concatenate(attended, axis=1)
     local[9].wait()
 
-    base = links.used
+    base = COPIES - 16
     own_cols = pl.ds(pl.multiple_of(g * GROUP, GROUP), GROUP)
     other_cols = pl.ds(pl.multiple_of((1 - g) * GROUP, GROUP), GROUP)
 
-    def term_copy(d, kind, step):
+    def term_copy(r, d, kind, step):
         return pltpu.make_async_remote_copy(
-            src_ref=z_out.at[d, :, (own_cols, other_cols)[kind]],
-            dst_ref=z_in.at[kind, step],
-            send_sem=send_sems.at[base + 4 * kind + step],
-            recv_sem=recv_sems.at[base + 4 * kind + step],
+            src_ref=z_out.at[r, d, :, (own_cols, other_cols)[kind]],
+            dst_ref=z_in.at[r, kind, step],
+            send_sem=send_sems.at[base + 8 * r + 4 * kind + step],
+            recv_sem=recv_sems.at[base + 8 * r + 4 * kind + step],
             device_id={"guide": (g, 1 - g)[kind], "tp": (t + step) % 4},
             device_id_type=pl.DeviceIdType.MESH,
         )
 
-    for d in (0, 1, 3, 2):
+    for d in range(4):
         e = (x + d) % 4
+        heads_term[d] = dot(attended, wout_v[:, pl.ds(pl.multiple_of(e * WIDE, WIDE), WIDE)])
+
+    def send_term(r, d):
         step = (x + d - t + 4) % 4
-        term = dot(attended, wout_v[:, pl.ds(pl.multiple_of(e * WIDE, WIDE), WIDE)])
+        term = heads_term[d, r * PART : (r + 1) * PART]
         if d == 0:
-            term += mlp_out[0].astype(F32)
+            term += mlp_out[r, 0].astype(F32)
         else:
-            mlp_sent[d].wait_recv()
-            term += mlp_in[d].astype(F32)
-        z_out[d] = term.astype(BF16)
-        term_copy(d, 1, step).start()
+            mlp_sent[r][d].wait_recv()
+            term += mlp_in[r, d].astype(F32)
+        z_out[r, d] = term.astype(BF16)
+        term_copy(r, d, 1, step).start()
 
         @pl.when(step != 0)
         def _():
-            term_copy(d, 0, step).start()
+            term_copy(r, d, 0, step).start()
+
+    send_term(0, 0)
+    mlp_sent.append(output_product(1))
+    for d in (1, 3, 2):
+        send_term(0, d)
+    for d in (0, 1, 3, 2):
+        send_term(1, d)
 
     gate_sent.wait_recv()
     own_table = mod_v[2, :, pl.ds(pl.multiple_of(t * WIDE + g * GROUP, GROUP), GROUP)].astype(F32)
@@ -451,21 +471,25 @@
         return found
 
     own_gate, other_gate = gate_of(own_table), gate_of(other_table)
-    residual = raw[0, 0, :, own_cols].astype(F32)
-    own_branch = z_out[(t - x + 4) % 4, :, own_cols].astype(F32)
-    arrived = [term_copy(0, 0, step) for step in (1, 2, 3)] + [term_copy(0, 1, step) for step in range(4)]
-    for made in arrived:
-        made.wait_recv()
-    for step in (1, 2, 3):
-        own_branch += z_in[0, step].astype(F32)
-    other_branch = z_in[1, 0].astype(F32)
-    for step in (1, 2, 3):
-        other_branch += z_in[1, step].astype(F32)
-    mine = (residual + own_gate * own_branch).astype(BF16).astype(F32)
-    theirs = (residual + other_gate * other_branch).astype(BF16).astype(F32)
-    cond = jnp.where(g == 0, mine, theirs)
-    uncond = jnp.where(g == 0, theirs, mine)
-    result[...] = (uncond + GUIDANCE * (cond - uncond)).astype(BF16)
+    arrived = []
+    for r in range(2):
+        rows = slice(r * PART, (r + 1) * PART)
+        residual = raw[0, 0, rows, own_cols].astype(F32)
+        own_branch = z_out[r, (t - x + 4) % 4, :, own_cols].astype(F32)
+        here = [term_copy(r, 0, 0, step) for step in (1, 2, 3)] + [term_copy(r, 0, 1, step) for step in range(4)]
+        for made in here:
+            made.wait_recv()
+        arrived += here
+        for step in (1, 2, 3):
+            own_branch += z_in[r, 0, step].astype(F32)
+        other_branch = z_in[r, 1, 0].astype(F32)
+        for step in (1, 2, 3):
+            other_branch += z_in[r, 1, step].astype(F32)
+        mine = (residual + own_gate[rows] * own_branch).astype(BF16).astype(F32)
+        theirs = (residual + other_gate[rows] * other_branch).astype(BF16).astype(F32)
+        cond = jnp.where(g == 0, mine, theirs)
+        uncond = jnp.where(g == 0, theirs, mine)
+        result[rows] = (uncond + GUIDANCE * (cond - uncond)).astype(BF16)
     for made in arrived:
         made.wait_send()
     links.drain()
@@ -493,11 +517,12 @@
             pltpu.VMEM((4 * ROWS, HEAD), BF16),
             pltpu.VMEM((4, ROWS, GROUP + HEAD), BF16),
             pltpu.VMEM((4, ROWS, GROUP + HEAD), BF16),
-            pltpu.VMEM((4, 4, ROWS, GROUP), BF16),
-            pltpu.VMEM((4, ROWS, WIDE), BF16),
-            pltpu.VMEM((4, ROWS, WIDE), BF16),
-            pltpu.VMEM((4, ROWS, WIDE), BF16),
-            pltpu.VMEM((2, 4, ROWS, GROUP), BF16),
+            pltpu.VMEM((4, 2, 4, PART, GROUP), BF16),
+            pltpu.VMEM((2, 4, PART, WIDE), BF16),
+            pltpu.VMEM((2, 4, PART, WIDE), BF16),
+            pltpu.VMEM((4, ROWS, WIDE), F32),
+            pltpu.VMEM((2, 4, PART, WIDE), BF16),
+            pltpu.VMEM((2, 2, 4, PART, GROUP), BF16),
             pltpu.VMEM((REQUESTS, GROUP), BF16),
             pltpu.SemaphoreType.DMA((COPIES,)),
             pltpu.SemaphoreType.DMA((COPIES,)),

time: 61.2 us -> 62 us (1.013)
  Pallas kernels: 59.6 us -> 60.5 us
    pallas_call x1, Pallas kernels: 59.6 us -> 60.5 us  [on_device(): pl.pallas_call(body, out_shape=jax.ShapeDtypeStruct((ROWS, GROUP), BF16),...]
where the time goes in v6:
time: 62 us; the launch traced here: 61.9 us
  Pallas kernels  60.5 us (98%)
  local copies, waits for them, and re-layouts  1.42 us (2%)
    pallas_call x1, Pallas kernels, on_device(): pl.pallas_call(body, out_shape=jax.ShapeDtypeStruct((ROWS, GROUP), BF16),...  60.5 us
    unnamed x1, local copies, waits for them, and re-layouts  1.42 us

profile of v6, /device:TPU:4, one launch (start us, length us, event | category | flops | bytes accessed | tf_op | source)
XLA Modules:
  0.0 61.9 jit_solution(771927531608961683)
XLA Ops:
  0.0 60.5 %layer.1 = bf16[64,384]{1,0:T(8,128)(2,1)} custom-call(bf16[64,768]{1,0:T(8,128)(2,1)} %hidden.1, s32[1,64]{1,0:T(1,128)} %bitcast.9, bf16[3,4,3072]{2,1,0:T(4,128)(2,1)} %bitcast.8, f32[2,128]{1,0:T(2,128)} %qk_gain.1, bf16[3,3072,384]{2,1,0:T(8,128)(2,1)} %bitcast.6, bf16[96,1536]{1,0:T(8,128)(2,1)} %w_in.1, bf16[384,3072]{1,0:T(8,128)(2,1)} %w_out.1, ...), custom_call_target="tpu_custom_call" | custom-call | tf_op jit(solution)/shard_map/layer/pallas_call | solution.py:500
  60.5 1.4 %copy.10 = bf16[64,1,1,384]{3,0,2,1:T(8,128)(2,1)} copy(bf16[64,1,1,384]{3,0,2,1:T(8,128)(2,1)} %bitcast.7) | data formatting | bytes 98304

commit v7 on v5

--- a/solution.py
+++ b/solution.py
@@ -204,6 +204,7 @@
     for made in win_sent:
         made.start()
     win_near.start()
+    wback_all.begin()
     over_x[0].start()
     for made in seg_sent:
         made.start()
@@ -228,10 +229,8 @@
     for made in seg_sent:
         made.wait_recv()
     win_rest.forward()
-    wback_all.begin()
-    local[7].wait()
-    win_near.finish()
-    over_first.start()
+    over_x[3].forward()
+    over_x[1].forward()
     over_tp.far()
     over_x[2].start()
 
@@ -269,8 +268,6 @@
             ).astype(BF16)
 
     normalise(0)
-    over_x[3].forward()
-    over_x[1].forward()
 
     def head_norm(values, gain):
         return values * lax.rsqrt(jnp.mean(values * values, axis=-1, keepdims=True) + 1e-06) * gain
@@ -281,21 +278,10 @@
     for h in range(HEADS_HERE):
         cols = slice(h * HEAD, (h + 1) * HEAD)
         kv[y, c, :, cols] = head_norm(keys[:, cols], gain_v[1:2, :]).astype(BF16)
-    win_sides.near()
-    over_sides[1].start()
-    over_sides[2].start()
     local[5].wait()
     kv[y, c, :, GROUP : 2 * GROUP] = dot(rows_own, wqkv_v[2]).astype(BF16)
     kv[y, c, :, 2 * GROUP :] = one_hots[0]
     kv_all.start()
-    over_x[2].forward()
-    win_rest.near()
-    over_rest[1].start()
-    over_rest[2].start()
-    win_sides.far()
-    over_sides[3].start()
-    win_rest.far()
-    over_rest[3].start()
     local[6].wait()
     query = dot(rows_own, wqkv_v[0])
     for h in range(HEADS_HERE):
@@ -303,18 +289,32 @@
         qx[0, :, cols] = head_norm(query[:, cols], gain_v[0:1, :]).astype(BF16)
     q_all.start()
 
+    over_x[2].forward()
+    local[7].wait()
+    win_near.finish()
+    over_first.start()
+    win_sides.near()
+    over_sides[1].start()
+    over_sides[2].start()
+    win_rest.near()
+    over_rest[1].start()
+    over_rest[2].start()
     kv_all.forward()
-    wback_all.follow()
     local[8].wait()
     over_back[0].start()
     wback_all.forward()
+    wback_all.follow()
+    win_sides.far()
+    over_sides[3].start()
+    win_rest.far()
+    over_rest[3].start()
+    q_all.forward()
     for k in (0, 1, 3, 2):
         over_x[k].finish()
     normalise(1)
-    q_all.forward()
-    normalise(3)
     kv_all.finish()
     kv_over.start()
+    normalise(3)
     normalise(2)
     for made in [over_first, *over_sides, *over_rest]:
         made.wait_recv()

time: 61.2 us -> 64.3 us (1.051)
  Pallas kernels: 59.6 us -> 62.8 us
    pallas_call x1, Pallas kernels: 59.6 us -> 62.8 us  [on_device(): pl.pallas_call(body, out_shape=jax.ShapeDtypeStruct((ROWS, GROUP), BF16),...]
where the time goes in v7:
time: 64.3 us; the launch traced here: 64.2 us
  Pallas kernels  62.8 us (98%)
  local copies, waits for them, and re-layouts  1.42 us (2%)
    pallas_call x1, Pallas kernels, on_device(): pl.pallas_call(body, out_shape=jax.ShapeDtypeStruct((ROWS, GROUP), BF16),...  62.8 us
    unnamed x1, local copies, waits for them, and re-layouts  1.42 us

profile of v7, /device:TPU:4, one launch (start us, length us, event | category | flops | bytes accessed | tf_op | source)
XLA Modules:
  0.0 64.2 jit_solution(18322175408489813640)
XLA Ops:
  0.0 62.8 %layer.1 = bf16[64,384]{1,0:T(8,128)(2,1)} custom-call(bf16[64,768]{1,0:T(8,128)(2,1)} %hidden.1, s32[1,64]{1,0:T(1,128)} %bitcast.9, bf16[3,4,3072]{2,1,0:T(4,128)(2,1)} %bitcast.8, f32[2,128]{1,0:T(2,128)} %qk_gain.1, bf16[3,3072,384]{2,1,0:T(8,128)(2,1)} %bitcast.6, bf16[96,1536]{1,0:T(8,128)(2,1)} %w_in.1, bf16[384,3072]{1,0:T(8,128)(2,1)} %w_out.1, ...), custom_call_target="tpu_custom_call" | custom-call | tf_op jit(solution)/shard_map/layer/pallas_call | solution.py:476
  62.8 1.4 %copy.10 = bf16[64,1,1,384]{3,0,2,1:T(8,128)(2,1)} copy(bf16[64,1,1,384]{3,0,2,1:T(8,128)(2,1)} %bitcast.7) | data formatting | bytes 98304

commit v8 on v5

--- a/solution.py
+++ b/solution.py
@@ -192,7 +192,7 @@
     over_rest = [to_mate(win.at[3, yy, c]) for yy in (y, yr, yl, (y + 2) % 4)]
     over_back = [to_mate(wback.at[yy, c]) for yy in (y, yr, yl, (y + 2) % 4)]
     kv_all = absolute(lambda yy, h: kv.at[yy, c, half32(h)])
-    kv_over = links.copy(kv.at[:, c], kv.at[:, c], mate)
+    over_kv = [to_mate(kv.at[yy, c]) for yy in (y, yr, yl, (y + 2) % 4)]
     q_all = relative(x_right, x_left, lambda d, h: qx.at[d, half32(h)])
     act_all = relative(x_right, x_left, lambda d, h: act.at[d, two(h)])
 
@@ -288,6 +288,7 @@
     kv[y, c, :, GROUP : 2 * GROUP] = dot(rows_own, wqkv_v[2]).astype(BF16)
     kv[y, c, :, 2 * GROUP :] = one_hots[0]
     kv_all.start()
+    over_kv[0].start()
     over_x[2].forward()
     win_rest.near()
     over_rest[1].start()
@@ -310,11 +311,14 @@
     wback_all.forward()
     for k in (0, 1, 3, 2):
         over_x[k].finish()
+    kv_all.near()
+    over_kv[1].start()
+    over_kv[2].start()
     normalise(1)
     q_all.forward()
     normalise(3)
-    kv_all.finish()
-    kv_over.start()
+    kv_all.far()
+    over_kv[3].start()
     normalise(2)
     for made in [over_first, *over_sides, *over_rest]:
         made.wait_recv()
@@ -329,7 +333,8 @@
     act_all.start()
 
     q_all.finish()
-    kv_over.wait_recv()
+    for made in over_kv:
+        made.wait_recv()
 
     seen = kv.reshape(8 * ROWS, KV)
     same = dot_t(jnp.concatenate(one_hots, axis=0), seen[:, 2 * GROUP :]) > 0.5

time: 61.2 us -> 63.2 us (1.033)
  the two profiles are of different devices: /device:TPU:4 before, /device:TPU:8 now
where the time goes in v8:
time: 63.2 us; the launch traced here: 63.1 us
  Pallas kernels  61.6 us (97%)
  local copies, waits for them, and re-layouts  1.42 us (2%)
    pallas_call x1, Pallas kernels, on_device(): pl.pallas_call(body, out_shape=jax.ShapeDtypeStruct((ROWS, GROUP), BF16),...  61.6 us
    unnamed x1, local copies, waits for them, and re-layouts  1.42 us

profile of v8, /device:TPU:8, one launch (start us, length us, event | category | flops | bytes accessed | tf_op | source)
XLA Modules:
  0.0 63.1 jit_solution(9734753666652208509)
XLA Ops:
  0.0 61.6 %layer.1 = bf16[64,384]{1,0:T(8,128)(2,1)} custom-call(bf16[64,768]{1,0:T(8,128)(2,1)} %hidden.1, s32[1,64]{1,0:T(1,128)} %bitcast.9, bf16[3,4,3072]{2,1,0:T(4,128)(2,1)} %bitcast.8, f32[2,128]{1,0:T(2,128)} %qk_gain.1, bf16[3,3072,384]{2,1,0:T(8,128)(2,1)} %bitcast.6, bf16[96,1536]{1,0:T(8,128)(2,1)} %w_in.1, bf16[384,3072]{1,0:T(8,128)(2,1)} %w_out.1, ...), custom_call_target="tpu_custom_call" | custom-call | tf_op jit(solution)/shard_map/layer/pallas_call | solution.py:481
  61.6 1.4 %copy.10 = bf16[64,1,1,384]{3,0,2,1:T(8,128)(2,1)} copy(bf16[64,1,1,384]{3,0,2,1:T(8,128)(2,1)} %bitcast.7) | data formatting | bytes 98304

commit v9 on v5

--- a/solution.py
+++ b/solution.py
@@ -228,7 +228,6 @@
     for made in seg_sent:
         made.wait_recv()
     win_rest.forward()
-    wback_all.begin()
     local[7].wait()
     win_near.finish()
     over_first.start()
@@ -288,6 +287,7 @@
     kv[y, c, :, GROUP : 2 * GROUP] = dot(rows_own, wqkv_v[2]).astype(BF16)
     kv[y, c, :, 2 * GROUP :] = one_hots[0]
     kv_all.start()
+    wback_all.begin()
     over_x[2].forward()
     win_rest.near()
     over_rest[1].start()

time: 61.2 us -> 63.4 us (1.036)
  Pallas kernels: 59.6 us -> 61.8 us
    pallas_call x1, Pallas kernels: 59.6 us -> 61.8 us  [on_device(): pl.pallas_call(body, out_shape=jax.ShapeDtypeStruct((ROWS, GROUP), BF16),...]
where the time goes in v9:
time: 63.4 us; the launch traced here: 63.2 us
  Pallas kernels  61.8 us (97%)
  local copies, waits for them, and re-layouts  1.42 us (2%)
    pallas_call x1, Pallas kernels, on_device(): pl.pallas_call(body, out_shape=jax.ShapeDtypeStruct((ROWS, GROUP), BF16),...  61.8 us
    unnamed x1, local copies, waits for them, and re-layouts  1.42 us

profile of v9, /device:TPU:4, one launch (start us, length us, event | category | flops | bytes accessed | tf_op | source)
XLA Modules:
  0.0 63.2 jit_solution(16388260456988031989)
XLA Ops:
  0.0 61.8 %layer.1 = bf16[64,384]{1,0:T(8,128)(2,1)} custom-call(bf16[64,768]{1,0:T(8,128)(2,1)} %hidden.1, s32[1,64]{1,0:T(1,128)} %bitcast.9, bf16[3,4,3072]{2,1,0:T(4,128)(2,1)} %bitcast.8, f32[2,128]{1,0:T(2,128)} %qk_gain.1, bf16[3,3072,384]{2,1,0:T(8,128)(2,1)} %bitcast.6, bf16[96,1536]{1,0:T(8,128)(2,1)} %w_in.1, bf16[384,3072]{1,0:T(8,128)(2,1)} %w_out.1, ...), custom_call_target="tpu_custom_call" | custom-call | tf_op jit(solution)/shard_map/layer/pallas_call | solution.py:476
  61.8 1.4 %copy.10 = bf16[64,1,1,384]{3,0,2,1:T(8,128)(2,1)} copy(bf16[64,1,1,384]{3,0,2,1:T(8,128)(2,1)} %bitcast.7) | data formatting | bytes 98304

commit v10 on v5

--- a/solution.py
+++ b/solution.py
@@ -355,8 +355,6 @@
             wback_all.near()
             over_back[1].start()
             over_back[2].start()
-        if h == 1:
-            act_all.forward()
     part_out[:, :, GROUP:] = stats.astype(BF16).reshape(4, ROWS, HEAD)
     part_sent = [
         links.copy(part_out.at[2], part_in.at[2], x_far),
@@ -365,6 +363,7 @@
     ]
     for made in part_sent:
         made.start()
+    act_all.forward()
     wback_all.far()
     over_back[3].start()
     for made in over_back:

time: 61.2 us -> 63.3 us (1.034)
  Pallas kernels: 59.6 us -> 61.7 us
    pallas_call x1, Pallas kernels: 59.6 us -> 61.7 us  [on_device(): pl.pallas_call(body, out_shape=jax.ShapeDtypeStruct((ROWS, GROUP), BF16),...]
where the time goes in v10:
time: 63.3 us; the launch traced here: 63.2 us
  Pallas kernels  61.7 us (97%)
  local copies, waits for them, and re-layouts  1.42 us (2%)
    pallas_call x1, Pallas kernels, on_device(): pl.pallas_call(body, out_shape=jax.ShapeDtypeStruct((ROWS, GROUP), BF16),...  61.7 us
    unnamed x1, local copies, waits for them, and re-layouts  1.42 us

profile of v10, /device:TPU:4, one launch (start us, length us, event | category | flops | bytes accessed | tf_op | source)
XLA Modules:
  0.0 63.2 jit_solution(3526248607798360857)
XLA Ops:
  0.0 61.7 %layer.1 = bf16[64,384]{1,0:T(8,128)(2,1)} custom-call(bf16[64,768]{1,0:T(8,128)(2,1)} %hidden.1, s32[1,64]{1,0:T(1,128)} %bitcast.9, bf16[3,4,3072]{2,1,0:T(4,128)(2,1)} %bitcast.8, f32[2,128]{1,0:T(2,128)} %qk_gain.1, bf16[3,3072,384]{2,1,0:T(8,128)(2,1)} %bitcast.6, bf16[96,1536]{1,0:T(8,128)(2,1)} %w_in.1, bf16[384,3072]{1,0:T(8,128)(2,1)} %w_out.1, ...), custom_call_target="tpu_custom_call" | custom-call | tf_op jit(solution)/shard_map/layer/pallas_call | solution.py:475
  61.7 1.4 %copy.10 = bf16[64,1,1,384]{3,0,2,1:T(8,128)(2,1)} copy(bf16[64,1,1,384]{3,0,2,1:T(8,128)(2,1)} %bitcast.7) | data formatting | bytes 98304

commit v11 on v5

--- a/solution.py
+++ b/solution.py
@@ -232,6 +232,8 @@
     local[7].wait()
     win_near.finish()
     over_first.start()
+    over_x[3].forward()
+    over_x[1].forward()
     over_tp.far()
     over_x[2].start()
 
@@ -269,8 +271,6 @@
             ).astype(BF16)
 
     normalise(0)
-    over_x[3].forward()
-    over_x[1].forward()
 
     def head_norm(values, gain):
         return values * lax.rsqrt(jnp.mean(values * values, axis=-1, keepdims=True) + 1e-06) * gain

time: 61.2 us -> 61.7 us (level)
  no operation moved by 1% of the time
where the time goes in v11:
time: 61.7 us; the launch traced here: 61.6 us
  Pallas kernels  60.1 us (97%)
  local copies, waits for them, and re-layouts  1.42 us (2%)
    pallas_call x1, Pallas kernels, on_device(): pl.pallas_call(body, out_shape=jax.ShapeDtypeStruct((ROWS, GROUP), BF16),...  60.1 us
    unnamed x1, local copies, waits for them, and re-layouts  1.42 us

profile of v11, /device:TPU:4, one launch (start us, length us, event | category | flops | bytes accessed | tf_op | source)
XLA Modules:
  0.0 61.6 jit_solution(12115929143391154168)
XLA Ops:
  0.0 60.1 %layer.1 = bf16[64,384]{1,0:T(8,128)(2,1)} custom-call(bf16[64,768]{1,0:T(8,128)(2,1)} %hidden.1, s32[1,64]{1,0:T(1,128)} %bitcast.9, bf16[3,4,3072]{2,1,0:T(4,128)(2,1)} %bitcast.8, f32[2,128]{1,0:T(2,128)} %qk_gain.1, bf16[3,3072,384]{2,1,0:T(8,128)(2,1)} %bitcast.6, bf16[96,1536]{1,0:T(8,128)(2,1)} %w_in.1, bf16[384,3072]{1,0:T(8,128)(2,1)} %w_out.1, ...), custom_call_target="tpu_custom_call" | custom-call | tf_op jit(solution)/shard_map/layer/pallas_call | solution.py:476
  60.1 1.4 %copy.10 = bf16[64,1,1,384]{3,0,2,1:T(8,128)(2,1)} copy(bf16[64,1,1,384]{3,0,2,1:T(8,128)(2,1)} %bitcast.7) | data formatting | bytes 98304
